TPU v7x, 128 devices: a whole 4x4x4 slice. The times are simulated.
128 devices in a mesh: row: 16 (over y, x_hi, core), col: 8 (over x_lo, z).
Axes of the slice: x: 4 (x_hi: 2, x_lo: 2; x = x_hi * 2 + x_lo), y: 4, z: 4, core: 2. Of those that a mesh axis runs over, the one named last changes fastest.
Arguments:
- field: bfloat16 [128, 128, 512], P('row', 'col'), may hold values from -6 to 6
- in_weight: bfloat16 [512, 2048], P(None, 'row'), may hold values from -0.25 to 0.25
- conv_weight: float32 [3, 3, 1024], replicated, may hold values from -2 to 2
- proj_weight: bfloat16 [1024, 256], replicated, may hold values from -0.1875 to 0.1875
- dt_weight: bfloat16 [4, 32, 1024], replicated, may hold values from -1 to 1
- dt_bias: float32 [4, 1024], replicated, may hold values from -7 to -2
- decay_rate: float32 [4, 16, 1024], replicated, may hold values from 0.5 to 2
- skip_gain: float32 [4, 1024], replicated, may hold values from 0.1 to 1.9
- norm_gain: float32 [1024], replicated, may hold values from 0.1 to 1.9
- out_weight: bfloat16 [1024, 512], P('col'), may hold values from -0.1875 to 0.1875
- grad_out: bfloat16 [128, 128, 512], P('row', 'col'), may hold values from -6 to 6
Outputs:
- result: bfloat16 [128, 128, 512], P('row', 'col')
- grad_field: float32 [128, 128, 512], P('row', 'col')
- grad_in_weight: float32 [512, 2048], P(None, 'row')
- grad_out_weight: float32 [1024, 512], P('col')
All inputs are finite; a program needn't handle non-finite values.
Results may differ from a plain program's by a relative error of at most 0.0073.
Values may be sent and summed in bfloat16 or wider, within the bound.
No kernel may reach another device: no remote copies, remote signals or barrier semaphores. Data moves between devices by JAX's collectives and lax.ppermute only.
A program may use at most 256 MiB of HBM per device.

v0:
```python
from functools import partial

import jax
import jax.numpy as jnp
from jax import lax
from jax.experimental import pallas as pl
from jax.experimental.pallas import tpu as pltpu
from jax.sharding import PartitionSpec as P

C = 512
E = 1024
N = 16
R = 32
K = 4
ROWS = 8
COLS = 16
CELLS = ROWS * COLS
LANES = 128
TILES = E // LANES
SLABS = CELLS // 8
WIDE = 512
GROUP = 8
LOG2E = 1.4426950408889634

DT_FLOOR = 0.004
NORM_EPS = 1e-05

F32 = jnp.float32
BF16 = jnp.bfloat16


def slab_rows(down, d, t):
    if down:
        half, p = divmod(t, ROWS)
        row = ROWS - 1 - p if d else p
        return pl.ds(row * COLS + half * 8, 8)
    col = COLS - 1 - t if d else t
    return pl.ds(col, 8, stride=COLS)


def chains(down):
    if down:
        return ((0, ROWS, 0), (ROWS, ROWS, 8))
    return ((0, COLS, 0),)


def split(v):
    high = v.astype(BF16)
    return high, (v - high.astype(F32)).astype(BF16)


def into_slabs(down, d, src, put):
    for t in range(SLABS):
        put(t, src[slab_rows(down, d, t), :])


def make_tables(down, proj_ref, psl_ref, tab_ref, first, count):
    for d in range(2):
        for t in range(SLABS):
            psl_ref[d, t * 8 : t * 8 + 8, :] = proj_ref[slab_rows(down, d, t), :]
        spread = psl_ref[d]
        for j in range(count):
            lane = d * (R + 2 * N) + first + j
            tab_ref[d, j] = jnp.broadcast_to(spread[:, lane : lane + 1], (CELLS, LANES))


def at_slab(t):
    if isinstance(t, int):
        return pl.ds(t * 8, 8)
    return pl.ds(pl.multiple_of(t * 8, 8), 8)


def spread_rates(rate_ref, d, nr_ref):
    for n in range(N):
        nr_ref[n] = jnp.broadcast_to(rate_ref[d, n : n + 1, :], (8, LANES))


def put_states(states, es_ref, out_ref, d, line):
    for n in range(N):
        es_ref[pl.ds(n, 8, stride=N), :] = states[n]
    for l in range(8):
        out_ref[line + l, d * N : (d + 1) * N, :] = es_ref[l * N : (l + 1) * N, :].astype(BF16)


def get_states(src_ref, es_ref, d, line):
    for l in range(8):
        es_ref[l * N : (l + 1) * N, :] = src_ref[line + l, d * N : (d + 1) * N, :].astype(F32)
    return [es_ref[pl.ds(n, 8, stride=N), :] for n in range(N)]


def walk(length, step, carry, backwards=False):
    def body(i, carry):
        for q in range(GROUP):
            at = i * GROUP + q
            carry = step(length - 1 - at if backwards else at, carry)
        return carry

    if length == GROUP:
        return body(0, carry)
    return lax.fori_loop(0, length // GROUP, body, carry)


def tree_sum(parts):
    while len(parts) > 1:
        parts = [sum(parts[i + 1 : i + 2], parts[i]) for i in range(0, len(parts), 2)]
    return parts[0]


def sums_kernel(
    active_ref, proj_ref, dtw_ref, bias_ref, rate_ref,
    ends_ref, step_ref, sig_ref,
    psl_ref, tab_ref, xf_ref, us_ref, nr_ref, es_ref, ts_ref,
    *, down,
):
    @pl.when(pl.program_id(0) == 0)
    def _():
        make_tables(down, proj_ref, psl_ref, tab_ref, R, N)

    xf_ref[...] = active_ref[...].astype(F32)
    for d in range(2):
        high, low = split(psl_ref[d])
        weights = dtw_ref[d]
        v = (
            jnp.dot(high, weights, preferred_element_type=F32)
            + jnp.dot(low, weights, preferred_element_type=F32)
            + bias_ref[d : d + 1, :]
        )
        small = jnp.exp(-jnp.abs(v))
        steps = DT_FLOOR + jnp.maximum(v, 0.0) + jnp.log(1.0 + small)
        step_ref[d] = steps
        sig_ref[d] = jnp.where(v >= 0.0, 1.0, small) / (1.0 + small)

        def put(t, x):
            us_ref[t * 8 : t * 8 + 8, :] = x * step_ref[d, t * 8 : t * 8 + 8, :]

        into_slabs(down, d, xf_ref, put)
        spread_rates(rate_ref, d, nr_ref)
        for first, length, line in chains(down):

            def step(p, carry):
                total, states = carry
                rows = at_slab(first + p)
                st = step_ref[d, rows, :]
                u = us_ref[rows, :]
                states = tuple(
                    jnp.exp2(st * nr_ref[n]) * states[n] + u * tab_ref[d, n, rows, :]
                    for n in range(N)
                )
                return total + st, states

            zero = jnp.zeros((8, LANES), F32)
            total, states = walk(length, step, (zero, (zero,) * N))
            put_states(states, es_ref, ends_ref, d, line)
            high = total.astype(BF16).astype(F32)
            ts_ref[pl.ds(line * 8 + 2 * d, 8, stride=8), :] = high
            ts_ref[pl.ds(line * 8 + 2 * d + 1, 8, stride=8), :] = total - high
    lines = COLS if down else ROWS
    for l in range(lines):
        ends_ref[l, 2 * N : 2 * N + 4, :] = ts_ref[l * 8 : l * 8 + 4, :].astype(BF16)


def outputs_kernel(
    active_ref, proj_ref, step_ref, rate_ref, skip_ref, start_ref,
    y_ref, hs_ref,
    psl_ref, tab_ref, xf_ref, us_ref, ys_ref, nr_ref, es_ref,
    *, down,
):
    @pl.when(pl.program_id(0) == 0)
    def _():
        make_tables(down, proj_ref, psl_ref, tab_ref, R, 2 * N)

    xf_ref[...] = active_ref[...].astype(F32)
    y_ref[...] = xf_ref[...] * skip_ref[...]
    for d in range(2):

        def put(t, x):
            us_ref[t * 8 : t * 8 + 8, :] = x * step_ref[d, t * 8 : t * 8 + 8, :]

        into_slabs(down, d, xf_ref, put)
        spread_rates(rate_ref, d, nr_ref)
        for at, (first, length, line) in enumerate(chains(down)):

            def step(p, states):
                rows = at_slab(first + p)
                st = step_ref[d, rows, :]
                u = us_ref[rows, :]
                kept = at_slab(first + at + p)
                for n in range(N):
                    hs_ref[d, n, kept, :] = states[n]
                states = tuple(
                    jnp.exp2(st * nr_ref[n]) * states[n] + u * tab_ref[d, n, rows, :]
                    for n in range(N)
                )
                parts = [states[n] * tab_ref[d, N + n, rows, :] for n in range(N)]
                ys_ref[rows, :] = tree_sum(parts)
                return states

            states = walk(length, step, tuple(get_states(start_ref, es_ref, d, line)))
            for n in range(N):
                hs_ref[d, n, at_slab(first + at + length), :] = states[n]
        for t in range(SLABS):
            rows = slab_rows(down, d, t)
            y_ref[rows, :] = y_ref[rows, :] + ys_ref[t * 8 : t * 8 + 8, :]


def back_sums_kernel(
    dy_ref, proj_ref, step_ref, rate_ref,
    ends_ref,
    psl_ref, tab_ref, dys_ref, nr_ref, es_ref,
    *, down,
):
    @pl.when(pl.program_id(0) == 0)
    def _():
        make_tables(down, proj_ref, psl_ref, tab_ref, R + N, N)

    for d in range(2):

        def put(t, x):
            dys_ref[t * 8 : t * 8 + 8, :] = x

        into_slabs(down, d, dy_ref, put)
        spread_rates(rate_ref, d, nr_ref)
        for first, length, line in chains(down):

            def step(p, states):
                rows = at_slab(first + p)
                st = step_ref[d, rows, :]
                dy = dys_ref[rows, :]
                return tuple(
                    jnp.exp2(st * nr_ref[n]) * (states[n] + dy * tab_ref[d, n, rows, :])
                    for n in range(N)
                )

            zero = jnp.zeros((8, LANES), F32)
            states = walk(length, step, (zero,) * N, backwards=True)
            put_states(states, es_ref, ends_ref, d, line)


def grads_kernel(
    active_ref, dy_ref, proj_ref, step_ref, sig_ref, rate_ref, skip_ref, dtw_ref, hs_ref, tail_ref,
    dx_ref, pg_ref,
    psl_ref, tab_ref, acc_ref, rank_ref, xf_ref, xs_ref, dys_ref, us_ref, dxs_ref, dvs_ref, nr_ref, es_ref,
    *, down,
):
    tile = pl.program_id(0)

    @pl.when(tile == 0)
    def _():
        make_tables(down, proj_ref, psl_ref, tab_ref, R, 2 * N)
        acc_ref[...] = jnp.zeros(acc_ref.shape, F32)
        rank_ref[...] = jnp.zeros(rank_ref.shape, F32)

    xf_ref[...] = active_ref[...].astype(F32)
    dx_ref[...] = dy_ref[...] * skip_ref[...]
    for d in range(2):

        def put(t, x):
            rows = slice(t * 8, t * 8 + 8)
            xs_ref[rows, :] = x
            us_ref[rows, :] = x * step_ref[d, rows, :]

        def put_dy(t, x):
            dys_ref[t * 8 : t * 8 + 8, :] = x

        into_slabs(down, d, xf_ref, put)
        into_slabs(down, d, dy_ref, put_dy)
        spread_rates(rate_ref, d, nr_ref)
        for at, (first, length, line) in enumerate(chains(down)):

            def backward(p, pulls):
                rows = at_slab(first + p)
                before = at_slab(first + at + p)
                after = at_slab(first + at + p + 1)
                st = step_ref[d, rows, :]
                u = us_ref[rows, :]
                dy = dys_ref[rows, :]
                back_u = []
                back_step = []
                new = []
                for n in range(N):
                    acc_ref[d, N + n, rows, :] += hs_ref[d, n, after, :] * dy
                    g = pulls[n] + dy * tab_ref[d, N + n, rows, :]
                    acc_ref[d, n, rows, :] += g * u
                    back_u.append(g * tab_ref[d, n, rows, :])
                    nr = nr_ref[n]
                    ag = jnp.exp2(st * nr) * g
                    back_step.append(ag * hs_ref[d, n, before, :] * nr)
                    new.append(ag)
                    if n % 4 == 3:
                        back_u = [tree_sum(back_u)]
                        back_step = [tree_sum(back_step)]
                back_u = back_u[0]
                dxs_ref[rows, :] = back_u * st
                dvs_ref[rows, :] = (back_step[0] * (1.0 / LOG2E) + back_u * xs_ref[rows, :]) * sig_ref[
                    d, rows, :
                ]
                return tuple(new)

            walk(length, backward, tuple(get_states(tail_ref, es_ref, d, line)), backwards=True)
        for t in range(SLABS):
            rows = slab_rows(down, d, t)
            dx_ref[rows, :] = dx_ref[rows, :] + dxs_ref[t * 8 : t * 8 + 8, :]
        high, low = split(dvs_ref[...])
        dims = (((1,), (1,)), ((), ()))
        rank_ref[d] += lax.dot_general(
            high, dtw_ref[d], dims, preferred_element_type=F32
        ) + lax.dot_general(low, dtw_ref[d], dims, preferred_element_type=F32)

    @pl.when(tile == TILES - 1)
    def _():
        for d in range(2):
            total = rank_ref[d]
            ones = jnp.ones((2 * LANES, LANES), BF16)
            column = lax.broadcasted_iota(jnp.int32, (CELLS, LANES), 1)
            for j in range(2 * N):
                lane = d * (R + 2 * N) + R + j
                both = jnp.concatenate(split(acc_ref[d, j]), axis=1)
                row_sums = jnp.dot(both, ones, preferred_element_type=F32)
                total = jnp.where(column == lane, row_sums, total)
            rank_ref[d] = total
            for t in range(SLABS):
                rows = slab_rows(down, d, t)
                piece = rank_ref[d, t * 8 : t * 8 + 8, :]
                pg_ref[rows, :] = pg_ref[rows, :] + piece if d else piece


def close_kernel(info_ref, ends_ref, rate_ref, out_ref, *, peers, flip):
    own = info_ref.shape[0] // peers
    for i in range(own):
        for d in range(2):
            order = [b * own + i for b in range(peers)]
            if (d == 1) != flip:
                order = order[::-1]
            nr = rate_ref[d]

            def total_of(b):
                return (
                    info_ref[b, 2 * N + 2 * d : 2 * N + 2 * d + 1, :].astype(F32)
                    + info_ref[b, 2 * N + 2 * d + 1 : 2 * N + 2 * d + 2, :].astype(F32)
                )

            def advance(state, b):
                end = ends_ref[b, d * N : (d + 1) * N, :].astype(F32)
                return jnp.exp2(nr * total_of(b)) * state + end

            state = jnp.zeros((N, WIDE), F32)
            loop = jnp.zeros((1, WIDE), F32)
            for b in order:
                state = advance(state, b)
                loop = loop + total_of(b)
            state = state / (1.0 - jnp.exp2(nr * loop))
            for b in order:
                out_ref[b, d * N : (d + 1) * N, :] = state.astype(BF16)
                state = advance(state, b)


def tail_kernel(y0_ref, y1_ref, gate_ref, gain_ref, back_ref, mixed_ref, back_sum_ref, back_gate_ref):
    summed = y0_ref[...] + y1_ref[...]
    centred = summed - jnp.mean(summed, axis=-1, keepdims=True)
    spread = jnp.mean(centred * centred, axis=-1, keepdims=True)
    scale = lax.rsqrt(spread + NORM_EPS)
    unit = centred * scale
    gain = gain_ref[...]
    normed = unit * gain
    gate = gate_ref[...].astype(F32)
    sig = 1.0 / (1.0 + jnp.exp(-gate))
    gated = gate * sig
    back = back_ref[...]
    mixed_ref[...] = (normed * gated).astype(BF16)
    back_gate_ref[...] = (back * normed * (sig + gated * (1.0 - sig))).astype(BF16)
    back_unit = back * gated * gain
    back_sum_ref[...] = scale * (
        back_unit
        - jnp.mean(back_unit, axis=-1, keepdims=True)
        - unit * jnp.mean(back_unit * unit, axis=-1, keepdims=True)
    )


def tiled(lead):
    zeros = (0,) * len(lead)
    return pl.BlockSpec((*lead, LANES), lambda i: (*zeros, i))


def by_tile(lead):
    zeros = (0,) * (len(lead) + 1)
    return pl.BlockSpec((None, *lead, LANES), lambda i: (i, *zeros))


def whole(shape):
    zeros = (0,) * len(shape)
    return pl.BlockSpec(shape, lambda i: zeros)


def vmem(*shape):
    return pltpu.VMEM(shape, F32)


PAIR = (2, CELLS)
PARAMS = pltpu.CompilerParams(dimension_semantics=("arbitrary",), vmem_limit_bytes=56 * 1024 * 1024)


def call(kernel, name, specs, outs, scratch, args):
    return pl.pallas_call(
        kernel,
        grid=(TILES,),
        in_specs=specs,
        out_specs=[spec for spec, _ in outs],
        out_shape=[jax.ShapeDtypeStruct(shape, dtype) for _, (shape, dtype) in outs],
        scratch_shapes=scratch,
        compiler_params=PARAMS,
        name=name,
    )(*args)


def block_sums(down, active, proj, dtw, bias, rates):
    lines = COLS if down else ROWS
    return call(
        partial(sums_kernel, down=down),
        "sums_down" if down else "sums_across",
        [tiled((CELLS,)), whole((CELLS, LANES)), tiled((2, LANES)), tiled((2,)), tiled((2, N))],
        [
            (tiled((lines, 2 * N + 4)), ((lines, 2 * N + 4, E), BF16)),
            (by_tile(PAIR), ((TILES, *PAIR, LANES), F32)),
            (by_tile(PAIR), ((TILES, *PAIR, LANES), F32)),
        ],
        [
            vmem(2, CELLS, LANES), vmem(2, N, CELLS, LANES), vmem(CELLS, LANES), vmem(CELLS, LANES),
            vmem(N, 8, LANES), vmem(8 * N, LANES), vmem(lines * 8, LANES),
        ],
        (active, proj, dtw, bias, rates),
    )


def kept_rows(down):
    return CELLS + 8 * len(chains(down))


def block_outputs(down, active, proj, steps, rates, skip, starts):
    lines = COLS if down else ROWS
    return call(
        partial(outputs_kernel, down=down),
        "outputs_down" if down else "outputs_across",
        [
            tiled((CELLS,)), whole((CELLS, LANES)), by_tile(PAIR), tiled((2, N)), tiled((1,)),
            tiled((lines, 2 * N)),
        ],
        [
            (tiled((CELLS,)), ((CELLS, E), F32)),
            (by_tile((2, N, kept_rows(down))), ((TILES, 2, N, kept_rows(down), LANES), F32)),
        ],
        [
            vmem(2, CELLS, LANES), vmem(2, 2 * N, CELLS, LANES), vmem(CELLS, LANES), vmem(CELLS, LANES),
            vmem(CELLS, LANES), vmem(N, 8, LANES), vmem(8 * N, LANES),
        ],
        (active, proj, steps, rates, skip, starts),
    )


def block_back_sums(down, back, proj, steps, rates):
    lines = COLS if down else ROWS
    return call(
        partial(back_sums_kernel, down=down),
        "back_sums_down" if down else "back_sums_across",
        [tiled((CELLS,)), whole((CELLS, LANES)), by_tile(PAIR), tiled((2, N))],
        [(tiled((lines, 2 * N)), ((lines, 2 * N, E), BF16))],
        [
            vmem(2, CELLS, LANES), vmem(2, N, CELLS, LANES), vmem(CELLS, LANES),
            vmem(N, 8, LANES), vmem(8 * N, LANES),
        ],
        (back, proj, steps, rates),
    )[0]


def block_grads(down, active, back, proj, steps, sigs, rates, skip, dtw, kept, tails):
    lines = COLS if down else ROWS
    cells = vmem(CELLS, LANES)
    return call(
        partial(grads_kernel, down=down),
        "grads_down" if down else "grads_across",
        [
            tiled((CELLS,)), tiled((CELLS,)), whole((CELLS, LANES)), by_tile(PAIR), by_tile(PAIR),
            tiled((2, N)), tiled((1,)), tiled((2, LANES)),
            by_tile((2, N, kept_rows(down))), tiled((lines, 2 * N)),
        ],
        [
            (tiled((CELLS,)), ((CELLS, E), F32)),
            (whole((CELLS, LANES)), ((CELLS, LANES), F32)),
        ],
        [
            vmem(2, CELLS, LANES), vmem(2, 2 * N, CELLS, LANES), vmem(2, 2 * N, CELLS, LANES),
            vmem(2, CELLS, LANES), cells, cells, cells, cells, cells, cells,
            vmem(N, 8, LANES), vmem(8 * N, LANES),
        ],
        (active, back, proj, steps, sigs, rates, skip, dtw, kept, tails),
    )


def closed(axis, info, ends, rates, flip):
    peers = lax.axis_size(axis)
    lines = info.shape[0]
    def wide(*lead):
        return pl.BlockSpec((*lead, WIDE), lambda i: (*(0,) * len(lead), i))

    return pl.pallas_call(
        partial(close_kernel, peers=peers, flip=flip),
        grid=(E // WIDE,),
        in_specs=[wide(*info.shape[:2]), wide(*ends.shape[:2]), wide(2, N)],
        out_specs=wide(lines, 2 * N),
        out_shape=jax.ShapeDtypeStruct((lines, 2 * N, E), BF16),
        compiler_params=PARAMS,
        name="close_" + axis,
    )(info, ends, rates)


def tail(y0, y1, gate, gain, back):
    rows = pl.BlockSpec((32, E), lambda i: (i, 0))
    return pl.pallas_call(
        tail_kernel,
        grid=(CELLS // 32,),
        in_specs=[rows, rows, rows, pl.BlockSpec((1, E), lambda i: (0, 0)), rows],
        out_specs=[rows, rows, rows],
        out_shape=[
            jax.ShapeDtypeStruct((CELLS, E), BF16),
            jax.ShapeDtypeStruct((CELLS, E), F32),
            jax.ShapeDtypeStruct((CELLS, E), BF16),
        ],
        compiler_params=PARAMS,
        name="tail",
    )(y0, y1, gate, gain, back)


def swapped(x, axis):
    return lax.all_to_all(x, axis, 0, 0, tiled=True)


def sent_to_all(shard, axis):
    peers = lax.axis_size(axis)
    return swapped(jnp.broadcast_to(shard[None], (peers, *shard.shape)), axis)


def across(shard):
    rows = lax.axis_size("row")
    return lax.ppermute(shard, "row", [(i, (i + rows // 2) % rows) for i in range(rows)])


def from_halves(pieces):
    pieces = pieces.reshape(2, 8, C // 2, LANES)
    return pieces.transpose(0, 2, 1, 3).reshape(C, E)


def owner_order(part):
    return part.astype(BF16).reshape(8, 2, 8, 8, C).transpose(1, 0, 2, 3, 4)


def reduced(pieces):
    pieces = lax.all_to_all(pieces.reshape(128, 8, C), ("row", "col"), 0, 0, tiled=True)
    return jnp.sum(pieces.astype(F32), axis=0)


def with_halo(cells, sides, width):
    for axis, dim in sides:
        count = lax.axis_size(axis)
        head = lax.slice_in_dim(cells, 0, width, axis=dim).astype(BF16)
        tail_part = lax.slice_in_dim(
            cells, cells.shape[dim] - width, cells.shape[dim], axis=dim
        ).astype(BF16)
        before = lax.ppermute(tail_part, axis, [(i, (i + 1) % count) for i in range(count)])
        after = lax.ppermute(head, axis, [((i + 1) % count, i) for i in range(count)])
        cells = jnp.concatenate(
            [before.astype(cells.dtype), cells, after.astype(cells.dtype)], axis=dim
        )
    return cells


def local(
    field,
    in_weight,
    conv_weight,
    proj_weight,
    dt_weight,
    dt_bias,
    decay_rate,
    skip_gain,
    norm_gain,
    out_weight,
    grad_out,
):
    upper = lax.axis_index("row") >= lax.axis_size("row") // 2
    first, last = in_weight[: C // 2], in_weight[C // 2 :]
    other = across(jnp.where(upper, first, last))
    in_source = sent_to_all(jnp.where(upper, other, first), "row")
    in_gate = jnp.where(upper, last, other)
    in_source, in_gate, out_weight = lax.optimization_barrier((in_source, in_gate, out_weight))
    in_source = from_halves(in_source)
    in_gate = from_halves(lax.all_gather(in_gate, "row"))
    out_full = lax.all_gather(out_weight, "col").reshape(E, C)
    field_rows = field.reshape(CELLS, C)
    grad_rows = grad_out.reshape(CELLS, C)
    field_wide = with_halo(field, (("row", 0), ("col", 1)), 1)
    padded = lax.dot_general(
        field_wide, in_source, (((2,), (0,)), ((), ())), preferred_element_type=F32
    ).astype(BF16)
    gate = jnp.dot(field_rows, in_gate, preferred_element_type=F32).astype(BF16)
    convolved = jnp.zeros((ROWS, COLS, E), F32)
    for a in range(3):
        for b in range(3):
            convolved = (
                convolved + padded[a : a + ROWS, b : b + COLS].astype(F32) * conv_weight[a, b]
            )
    convolved = convolved.reshape(CELLS, E)
    active = jax.nn.silu(convolved).astype(BF16)
    projected = jnp.dot(active, proj_weight, preferred_element_type=F32)
    back_mixed = lax.dot_general(
        grad_rows, out_full, (((1,), (1,)), ((), ())), preferred_element_type=F32
    )

    kinds = ((True, "row", 0), (False, "col", 2))
    width = R + 2 * N
    pads = [
        jnp.stack(
            [
                jnp.pad(dt_weight[k + d], ((d * width, LANES - R - d * width), (0, 0)))
                for d in range(2)
            ]
        )
        for _, _, k in kinds
    ]
    projs = [projected[:, k * width : k * width + LANES] for _, _, k in kinds]
    rates = [decay_rate[k : k + 2] * -LOG2E for _, _, k in kinds]
    skips = [skip_gain[k : k + 1] + skip_gain[k + 1 : k + 2] for _, _, k in kinds]

    sums = [
        block_sums(down, active, projs[i], pads[i], dt_bias[k : k + 2], rates[i])
        for i, (down, _, k) in enumerate(kinds)
    ]
    infos = [swapped(sums[i][0], axis) for i, (_, axis, _) in enumerate(kinds)]
    starts = [
        swapped(closed(axis, infos[i], infos[i], rates[i], False), axis)
        for i, (_, axis, _) in enumerate(kinds)
    ]
    outs = [
        block_outputs(down, active, projs[i], sums[i][1], rates[i], skips[i], starts[i])
        for i, (down, _, _) in enumerate(kinds)
    ]
    mixed, back_summed, back_gate = tail(outs[0][0], outs[1][0], gate, norm_gain[None], back_mixed)
    result = (
        field_rows.astype(F32) + jnp.dot(mixed, out_full, preferred_element_type=F32)
    ).astype(BF16)
    out_part = lax.dot_general(
        mixed, grad_rows, (((0,), (0,)), ((), ())), preferred_element_type=F32
    )
    gate_part = lax.dot_general(
        back_gate, field_rows, (((0,), (0,)), ((), ())), preferred_element_type=F32
    )

    back_ends = [
        swapped(block_back_sums(down, back_summed, projs[i], sums[i][1], rates[i]), axis)
        for i, (down, axis, _) in enumerate(kinds)
    ]
    tails = [
        swapped(closed(axis, infos[i], back_ends[i], rates[i], True), axis)
        for i, (_, axis, _) in enumerate(kinds)
    ]
    out_pieces = out_part.astype(BF16).reshape(8, 16, 8, C).transpose(1, 0, 2, 3)
    out_pieces, tails = lax.optimization_barrier((out_pieces, tails))
    out_piece = reduced(out_pieces)
    grads_of = [
        partial(
            block_grads, down, active, back_summed, projs[i], sums[i][1], sums[i][2], rates[i],
            skips[i], pads[i], outs[i][1],
        )
        for i, (down, _, _) in enumerate(kinds)
    ]
    grads = [grads_of[0](tails[0])]
    out_piece, gate_pieces, grads[0], tails[1] = lax.optimization_barrier(
        (out_piece, owner_order(gate_part), grads[0], tails[1])
    )
    gate_piece = reduced(gate_pieces)
    grads.append(grads_of[1](tails[1]))
    out_piece, gate_piece, grads = lax.optimization_barrier((out_piece, gate_piece, grads))
    grad_out_weight = sent_to_all(out_piece, "row").reshape(E // 8, C)
    proj_grads = jnp.concatenate([grads[0][1], grads[1][1]], axis=1)
    high, low = split(proj_grads)
    dims = (((1,), (1,)), ((), ()))
    back_active = (
        grads[0][0]
        + grads[1][0]
        + lax.dot_general(high, proj_weight, dims, preferred_element_type=F32)
        + lax.dot_general(low, proj_weight, dims, preferred_element_type=F32)
    )
    sig = jax.nn.sigmoid(convolved)
    back_conv = back_active * (sig + convolved * sig * (1.0 - sig))
    wide = with_halo(back_conv.reshape(ROWS, COLS, E), (("row", 0), ("col", 1)), 1)
    back_source = jnp.zeros((ROWS, COLS, E), F32)
    for a in range(3):
        for b in range(3):
            back_source = (
                back_source + wide[2 - a : 2 - a + ROWS, 2 - b : 2 - b + COLS] * conv_weight[a, b]
            )
    back_source = back_source.reshape(CELLS, E).astype(BF16)
    source_part = lax.dot_general(
        back_source, field_rows, (((0,), (0,)), ((), ())), preferred_element_type=F32
    )
    source_piece = reduced(owner_order(source_part))
    dims = (((1,), (1,)), ((), ()))
    grad_field = (
        grad_rows.astype(F32)
        + lax.dot_general(back_gate, in_gate, dims, preferred_element_type=F32)
        + lax.dot_general(back_source, in_source, dims, preferred_element_type=F32)
    )
    own = jnp.where(upper, gate_piece, source_piece)
    given = across(jnp.where(upper, source_piece, gate_piece))
    pair = jnp.where(upper, jnp.stack([given, own]), jnp.stack([own, given])).astype(BF16)
    grad_in_weight = (
        sent_to_all(pair, "col").transpose(1, 0, 2, 3).reshape(LANES, C).T.astype(F32)
    )
    return (
        result.reshape(ROWS, COLS, C),
        grad_field.reshape(ROWS, COLS, C),
        grad_in_weight,
        grad_out_weight,
    )


def solution(mesh):
    in_specs = (
        P("row", "col", None),
        P(None, "row"),
        P(),
        P(),
        P(),
        P(),
        P(),
        P(),
        P(),
        P("col", None),
        P("row", "col", None),
    )
    out_specs = (P("row", "col", None), P("row", "col", None), P(None, "row"), P("col", None))
    return jax.shard_map(local, mesh=mesh, in_specs=in_specs, out_specs=out_specs, check_vma=False)
```

profile of v0, /device:TPU:0, one launch (start us, length us, event | category | flops | bytes accessed | tf_op | source)
XLA Modules:
  0.0 387.9 jit_solution(10571418920903546569)
XLA Ops:
  12.3 5.4 %collective-permute-start.1 = (bf16[1,16,512]{2,1,0:T(8,128)(2,1)S(1)}, bf16[1,16,512]{2,1,0:T(8,128)(2,1)S(1)}, u32[]{:S(2)}, u32[]{:S(2)}) collective-permute-start(bf16[1,16,512]{2,1,0:T(8,128)(2,1)S(1)} %get-tuple-element.105), channel_id=1, source_target_pairs={{8,0},{16,8},{24,16},{32,24},{40,32},{48,40},{56,48},{64,56},{72,6... | collective-permute-start | bytes 49160 | tf_op jit(solution)/shard_map/ppermute | solution.py:568
  24.0 3.7 all-to-all-start
  28.5 5.0 %collective-permute-start.3 = (bf16[10,1,512]{2,1,0:T(2,128)(2,1)S(1)}, bf16[10,1,512]{2,1,0:T(2,128)(2,1)S(1)}, u32[]{:S(2)}, u32[]{:S(2)}) collective-permute-start(bf16[10,1,512]{2,1,0:T(2,128)(2,1)S(1)} %get-tuple-element.102), channel_id=1, source_target_pairs={{1,0},{2,1},{3,2},{4,3},{5,4},{6,5},{7,6},{0,7},{9,8},{10,9},{11,1... | collective-permute-start | bytes 30728 | tf_op jit(solution)/shard_map/ppermute | solution.py:568
  34.4 11.4 %all-to-all-done = bf16[16,256,128]{2,1,0:T(8,128)(2,1)S(1)} async-done(((bf16[16,256,128]{2,1,0:T(8,128)(2,1)}), bf16[16,256,128]{2,1,0:T(8,128)(2,1)S(1)}, u32[]{:S(2)}, u32[]{:S(2)}) %all-to-all-start) | async-done | bytes 1048608 | tf_op jit(solution)/shard_map/all_to_all | solution.py:533
  50.1 9.4 %sums_across.1 = (bf16[8,36,1024]{2,1,0:T(8,128)(2,1)}, f32[8,2,128,128]{3,2,1,0:T(8,128)}, f32[8,2,128,128]{3,2,1,0:T(8,128)}) custom-call(bf16[128,1024]{1,0:T(8,128)(2,1)} %copy-done.2, f32[128,128]{1,0:T(8,128)} %get-tuple-element.103.proj_ref, bf16[2,128,1024]{2,1,0:T(8,128)(2,1)} %pad_maximum_fusion.4.dtw_ref, f32[2,1024]{1,0:T(2,128)} %get-tuple-element.120.bias_ref, ...), custom_call_target="tpu_custom_call" | custom-call | tf_op jit(solution)/shard_map/sums_across/pallas_call | solution.py:403
  59.5 6.3 %all-to-all-start.3 = ((bf16[8,36,1024]{2,1,0:T(8,128)(2,1)}), bf16[8,36,1024]{2,1,0:T(8,128)(2,1)S(1)}, u32[]{:S(2)}, u32[]{:S(2)}) async-start(bf16[8,36,1024]{2,1,0:T(8,128)(2,1)} %get-tuple-element.43), calls=%async_computation.3 | async-start | bytes 1310720 | tf_op jit(solution)/shard_map/all_to_all | solution.py:533
  66.7 8.8 %sums_down.1 = (bf16[16,36,1024]{2,1,0:T(8,128)(2,1)}, f32[8,2,128,128]{3,2,1,0:T(8,128)}, f32[8,2,128,128]{3,2,1,0:T(8,128)}) custom-call(bf16[128,1024]{1,0:T(8,128)(2,1)} %copy-done.2, f32[128,128]{1,0:T(8,128)} %get-tuple-element.104.proj_ref, bf16[2,128,1024]{2,1,0:T(8,128)(2,1)} %pad_maximum_fusion.3.dtw_ref, f32[2,1024]{1,0:T(2,128)} %get-tuple-element.121.bias_ref, ...), custom_call_target="tpu_custom_call" | custom-call | tf_op jit(solution)/shard_map/sums_down/pallas_call | solution.py:403
  78.7 4.0 %all-to-all-start.1 = ((bf16[16,36,1024]{2,1,0:T(8,128)(2,1)}), bf16[16,36,1024]{2,1,0:T(8,128)(2,1)S(1)}, u32[]{:S(2)}, u32[]{:S(2)}) async-start(bf16[16,36,1024]{2,1,0:T(8,128)(2,1)} %get-tuple-element.40), calls=%async_computation.1 | async-start | bytes 2621440 | tf_op jit(solution)/shard_map/all_to_all | solution.py:533
  85.8 17.7 %all-to-all-done.1.info_ref.ends_ref = bf16[16,36,1024]{2,1,0:T(8,128)(2,1)S(1)} async-done(((bf16[16,36,1024]{2,1,0:T(8,128)(2,1)}), bf16[16,36,1024]{2,1,0:T(8,128)(2,1)S(1)}, u32[]{:S(2)}, u32[]{:S(2)}) %all-to-all-start.1) | async-done | bytes 1179680 | tf_op jit(solution)/shard_map/all_to_all | solution.py:533
  110.4 6.2 %all-to-all-done.4.start_ref = bf16[8,32,1024]{2,1,0:T(8,128)(2,1)S(1)} async-done(((bf16[8,32,1024]{2,1,0:T(8,128)(2,1)}), bf16[8,32,1024]{2,1,0:T(8,128)(2,1)S(1)}, u32[]{:S(2)}, u32[]{:S(2)}) %all-to-all-start.4) | async-done | bytes 524320 | tf_op jit(solution)/shard_map/all_to_all | solution.py:533
  117.4 3.8 all-to-all-start.2
  121.8 11.9 %outputs_across.1 = (f32[128,1024]{1,0:T(8,128)}, f32[8,2,16,136,128]{4,3,2,1,0:T(8,128)}) custom-call(bf16[128,1024]{1,0:T(8,128)(2,1)} %copy-done.2, f32[128,128]{1,0:T(8,128)} %get-tuple-element.103.proj_ref, f32[8,2,128,128]{3,2,1,0:T(8,128)} %get-tuple-element.42.step_ref, f32[2,16,1024]{2,1,0:T(8,128)} %get-tuple-element.93.rate_ref, ...), custom_call_target="tpu_custom_call" | custom-call | tf_op jit(solution)/shard_map/outputs_across/pallas_call | solution.py:403
  143.1 12.0 %outputs_down.1 = (f32[128,1024]{1,0:T(8,128)}, f32[8,2,16,144,128]{4,3,2,1,0:T(8,128)}) custom-call(bf16[128,1024]{1,0:T(8,128)(2,1)} %copy-done.2, f32[128,128]{1,0:T(8,128)} %get-tuple-element.104.proj_ref, f32[8,2,128,128]{3,2,1,0:T(8,128)} %get-tuple-element.39.step_ref, f32[2,16,1024]{2,1,0:T(8,128)} %get-tuple-element.94.rate_ref, ...), custom_call_target="tpu_custom_call" | custom-call | tf_op jit(solution)/shard_map/outputs_down/pallas_call | solution.py:403
  155.1 4.1 %tail.1 = (bf16[128,1024]{1,0:T(8,128)(2,1)}, f32[128,1024]{1,0:T(8,128)}, bf16[128,1024]{1,0:T(8,128)(2,1)}) custom-call(f32[128,1024]{1,0:T(8,128)} %get-tuple-element.41.y0_ref, f32[128,1024]{1,0:T(8,128)} %get-tuple-element.44.y1_ref, bf16[128,1024]{1,0:T(8,128)(2,1)} %fusion.1.gate_ref, f32[1,1024]{1,0:T(1,128)} %bitcast.159, ...), custom_call_target="tpu_custom_call" | custom-call | tf_op jit(solution)/shard_map/tail/pallas_call | solution.py:517
  159.2 7.7 %back_sums_across.1 = bf16[8,32,1024]{2,1,0:T(8,128)(2,1)} custom-call(f32[128,1024]{1,0:T(8,128)} %get-tuple-element.49.dy_ref, f32[128,128]{1,0:T(8,128)} %get-tuple-element.103.proj_ref, f32[8,2,128,128]{3,2,1,0:T(8,128)} %get-tuple-element.42.step_ref, f32[2,16,1024]{2,1,0:T(8,128)} %get-tuple-element.93.rate_ref), custom_call_target="tpu_custom_call" | custom-call | tf_op jit(solution)/shard_map/back_sums_across/pallas_call | solution.py:403
  166.8 4.2 %all-to-all-start.7 = ((bf16[8,32,1024]{2,1,0:T(8,128)(2,1)}), bf16[8,32,1024]{2,1,0:T(8,128)(2,1)S(1)}, u32[]{:S(2)}, u32[]{:S(2)}) async-start(bf16[8,32,1024]{2,1,0:T(8,128)(2,1)} %back_sums_across.1), calls=%async_computation.7 | async-start | bytes 1048576 | tf_op jit(solution)/shard_map/all_to_all | solution.py:533
  171.1 7.5 %back_sums_down.1 = bf16[16,32,1024]{2,1,0:T(8,128)(2,1)} custom-call(f32[128,1024]{1,0:T(8,128)} %get-tuple-element.49.dy_ref, f32[128,128]{1,0:T(8,128)} %get-tuple-element.104.proj_ref, f32[8,2,128,128]{3,2,1,0:T(8,128)} %get-tuple-element.39.step_ref, f32[2,16,1024]{2,1,0:T(8,128)} %get-tuple-element.94.rate_ref), custom_call_target="tpu_custom_call" | custom-call | tf_op jit(solution)/shard_map/back_sums_down/pallas_call | solution.py:403
  180.9 6.5 %all-to-all-start.5 = ((bf16[16,32,1024]{2,1,0:T(8,128)(2,1)}), bf16[16,32,1024]{2,1,0:T(8,128)(2,1)S(1)}, u32[]{:S(2)}, u32[]{:S(2)}) async-start(bf16[16,32,1024]{2,1,0:T(8,128)(2,1)} %back_sums_down.1), calls=%async_computation.5 | async-start | bytes 2097152 | tf_op jit(solution)/shard_map/all_to_all | solution.py:533
  189.7 15.7 %all-to-all-done.5.ends_ref = bf16[16,32,1024]{2,1,0:T(8,128)(2,1)S(1)} async-done(((bf16[16,32,1024]{2,1,0:T(8,128)(2,1)}), bf16[16,32,1024]{2,1,0:T(8,128)(2,1)S(1)}, u32[]{:S(2)}, u32[]{:S(2)}) %all-to-all-start.5) | async-done | bytes 1048608 | tf_op jit(solution)/shard_map/all_to_all | solution.py:533
  212.0 6.3 %all-to-all-done.8.tail_ref = bf16[8,32,1024]{2,1,0:T(8,128)(2,1)S(1)} async-done(((bf16[8,32,1024]{2,1,0:T(8,128)(2,1)}), bf16[8,32,1024]{2,1,0:T(8,128)(2,1)S(1)}, u32[]{:S(2)}, u32[]{:S(2)}) %all-to-all-start.8) | async-done | bytes 524320 | tf_op jit(solution)/shard_map/all_to_all | solution.py:533
  218.3 3.7 all-to-all-start.6
  224.5 15.5 %all-to-all-done.6.tail_ref = bf16[16,32,1024]{2,1,0:T(8,128)(2,1)S(1)} async-done(((bf16[16,32,1024]{2,1,0:T(8,128)(2,1)}), bf16[16,32,1024]{2,1,0:T(8,128)(2,1)S(1)}, u32[]{:S(2)}, u32[]{:S(2)}) %all-to-all-start.6) | async-done | bytes 1048608 | tf_op jit(solution)/shard_map/all_to_all | solution.py:533
  239.9 6.1 %all-to-all-start.9 = ((bf16[128,8,512]{2,1,0:T(8,128)(2,1)}), bf16[128,8,512]{2,1,0:T(8,128)(2,1)}, u32[]{:S(2)}, u32[]{:S(2)}) async-start(bf16[128,8,512]{2,1,0:T(8,128)(2,1)} %bitcast.122), calls=%async_computation.9 | async-start | bytes 2097152 | tf_op jit(solution)/shard_map/all_to_all | solution.py:556
  247.6 20.4 %grads_down.1 = (f32[128,1024]{1,0:T(8,128)}, f32[128,128]{1,0:T(8,128)}) custom-call(bf16[128,1024]{1,0:T(8,128)(2,1)} %copy-done.2, f32[128,1024]{1,0:T(8,128)} %get-tuple-element.49.dy_ref, f32[128,128]{1,0:T(8,128)} %get-tuple-element.104.proj_ref, f32[8,2,128,128]{3,2,1,0:T(8,128)} %get-tuple-element.39.step_ref, ...), custom_call_target="tpu_custom_call" | custom-call | tf_op jit(solution)/shard_map/grads_down/pallas_call | solution.py:403
  269.4 9.5 %all-to-all-start.10 = ((bf16[128,8,512]{2,1,0:T(8,128)(2,1)}), bf16[128,8,512]{2,1,0:T(8,128)(2,1)S(1)}, u32[]{:S(2)}, u32[]{:S(2)}) async-start(bf16[128,8,512]{2,1,0:T(8,128)(2,1)} %bitcast.33), calls=%async_computation.10 | async-start | bytes 2097152 | tf_op jit(solution)/shard_map/all_to_all | solution.py:556
  278.9 24.2 %grads_across.1 = (f32[128,1024]{1,0:T(8,128)}, f32[128,128]{1,0:T(8,128)}) custom-call(bf16[128,1024]{1,0:T(8,128)(2,1)} %copy-done.2, f32[128,1024]{1,0:T(8,128)} %get-tuple-element.49.dy_ref, f32[128,128]{1,0:T(8,128)} %get-tuple-element.103.proj_ref, f32[8,2,128,128]{3,2,1,0:T(8,128)} %get-tuple-element.42.step_ref, ...), custom_call_target="tpu_custom_call" | custom-call | tf_op jit(solution)/shard_map/grads_across/pallas_call | solution.py:403
  307.6 4.5 %collective-permute-start.6 = (bf16[1,16,1024]{2,1,0:T(8,128)(2,1)S(1)}, bf16[1,16,1024]{2,1,0:T(8,128)(2,1)S(1)}, u32[]{:S(2)}, u32[]{:S(2)}) collective-permute-start(bf16[1,16,1024]{2,1,0:T(8,128)(2,1)S(1)} %get-tuple-element.92), channel_id=1, source_target_pairs={{8,0},{16,8},{24,16},{32,24},{40,32},{48,40},{56,48},{64,56},{72,6... | collective-permute-start | bytes 98312 | tf_op jit(solution)/shard_map/ppermute | solution.py:568
  313.6 5.3 %collective-permute-done.5 = bf16[1,16,1024]{2,1,0:T(8,128)(2,1)S(1)} collective-permute-done((bf16[1,16,1024]{2,1,0:T(8,128)(2,1)S(1)}, bf16[1,16,1024]{2,1,0:T(8,128)(2,1)S(1)}, u32[]{:S(2)}, u32[]{:S(2)}) %collective-permute-start.5) | collective-permute-done | bytes 32800 | tf_op jit(solution)/shard_map/ppermute | solution.py:567
  324.3 4.4 %collective-permute-done.8 = bf16[10,1,1024]{2,1,0:T(2,128)(2,1)S(1)} collective-permute-done((bf16[10,1,1024]{2,1,0:T(2,128)(2,1)S(1)}, bf16[10,1,1024]{2,1,0:T(2,128)(2,1)S(1)}, u32[]{:S(2)}, u32[]{:S(2)}) %collective-permute-start.8) | collective-permute-done | bytes 20512 | tf_op jit(solution)/shard_map/ppermute | solution.py:567
  331.0 5.8 %all-to-all-start.11 = ((bf16[128,8,512]{2,1,0:T(8,128)(2,1)}), bf16[128,8,512]{2,1,0:T(8,128)(2,1)}, u32[]{:S(2)}, u32[]{:S(2)}) async-start(bf16[128,8,512]{2,1,0:T(8,128)(2,1)} %bitcast.42), calls=%async_computation.11 | async-start | bytes 2097152 | tf_op jit(solution)/shard_map/all_to_all | solution.py:556
  339.4 15.8 %all-to-all-done.11 = bf16[128,8,512]{2,1,0:T(8,128)(2,1)} async-done(((bf16[128,8,512]{2,1,0:T(8,128)(2,1)}), bf16[128,8,512]{2,1,0:T(8,128)(2,1)}, u32[]{:S(2)}, u32[]{:S(2)}) %all-to-all-start.11) | async-done | bytes 1048608 | tf_op jit(solution)/shard_map/all_to_all | solution.py:556
  375.1 4.4 %all-to-all-done.12 = bf16[8,2,8,512]{3,2,1,0:T(8,128)(2,1)S(1)} async-done(((bf16[8,2,8,512]{3,2,1,0:T(8,128)(2,1)}), bf16[8,2,8,512]{3,2,1,0:T(8,128)(2,1)S(1)}, u32[]{:S(2)}, u32[]{:S(2)}) %all-to-all-start.12) | async-done | bytes 131104 | tf_op jit(solution)/shard_map/all_to_all | solution.py:533
  (173 shorter events, 96.2 us)
Async XLA Ops:
  7.2 42.0 %copy-start = (bf16[1024,256]{1,0:T(8,128)(2,1)S(1)}, bf16[1024,256]{1,0:T(8,128)(2,1)}, u32[]{:S(2)}) copy-start(bf16[1024,256]{1,0:T(8,128)(2,1)} %param.14) | copy-start | bytes 1572868
  8.1 13.2 %collective-permute-start.4 = (bf16[256,128]{1,0:T(8,128)(2,1)S(1)}, bf16[256,128]{1,0:T(8,128)(2,1)S(1)}, u32[]{:S(2)}, u32[]{:S(2)}) collective-permute-start(bf16[256,128]{1,0:T(8,128)(2,1)S(1)} %broadcast_select_fusion.2), channel_id=1, source_target_pairs={{0,64},{8,72},{16,80},{24,88},{32,96},{40,104},{48,112},{56,120},{... | collective-permute-start | bytes 196616 | tf_op jit(solution)/shard_map/ppermute | solution.py:543
  12.3 16.2 %collective-permute-start = (bf16[1,16,512]{2,1,0:T(8,128)(2,1)S(1)}, bf16[1,16,512]{2,1,0:T(8,128)(2,1)S(1)}, u32[]{:S(2)}, u32[]{:S(2)}) collective-permute-start(bf16[1,16,512]{2,1,0:T(8,128)(2,1)S(1)} %get-tuple-element.106), channel_id=1, source_target_pairs={{0,8},{8,16},{16,24},{24,32},{32,40},{40,48},{48,56},{56,64},{64,7... | collective-permute-start | bytes 49160 | tf_op jit(solution)/shard_map/ppermute | solution.py:567
  12.3 16.2 %collective-permute-start.1 = (bf16[1,16,512]{2,1,0:T(8,128)(2,1)S(1)}, bf16[1,16,512]{2,1,0:T(8,128)(2,1)S(1)}, u32[]{:S(2)}, u32[]{:S(2)}) collective-permute-start(bf16[1,16,512]{2,1,0:T(8,128)(2,1)S(1)} %get-tuple-element.105), channel_id=1, source_target_pairs={{8,0},{16,8},{24,16},{32,24},{40,32},{48,40},{56,48},{64,56},{72,6... | collective-permute-start | bytes 49160 | tf_op jit(solution)/shard_map/ppermute | solution.py:568
  21.2 26.3 %copy-start.20 = (f32[1,1,1024]{2,1,0:T(1,128)}, f32[1,1,1024]{2,1,0:T(1,128)S(1)}, u32[]{:S(2)}) copy-start(f32[1,1,1024]{2,1,0:T(1,128)S(1)} %get-tuple-element.107) | copy-start | bytes 12292
  21.2 26.3 %copy-start.22 = (f32[1,1,1024]{2,1,0:T(1,128)}, f32[1,1,1024]{2,1,0:T(1,128)S(1)}, u32[]{:S(2)}) copy-start(f32[1,1,1024]{2,1,0:T(1,128)S(1)} %get-tuple-element.108) | copy-start | bytes 12292
  21.2 26.3 %copy-start.24 = (f32[1,1,1024]{2,1,0:T(1,128)}, f32[1,1,1024]{2,1,0:T(1,128)S(1)}, u32[]{:S(2)}) copy-start(f32[1,1,1024]{2,1,0:T(1,128)S(1)} %get-tuple-element.109) | copy-start | bytes 12292
  21.2 26.3 %copy-start.26 = (f32[1,1,1024]{2,1,0:T(1,128)}, f32[1,1,1024]{2,1,0:T(1,128)S(1)}, u32[]{:S(2)}) copy-start(f32[1,1,1024]{2,1,0:T(1,128)S(1)} %get-tuple-element.110) | copy-start | bytes 12292
  24.0 21.8 %all-to-all-start = ((bf16[16,256,128]{2,1,0:T(8,128)(2,1)}), bf16[16,256,128]{2,1,0:T(8,128)(2,1)S(1)}, u32[]{:S(2)}, u32[]{:S(2)}) async-start(bf16[16,256,128]{2,1,0:T(8,128)(2,1)} %broadcast_in_dim.8), calls=%async_computation | async-start | bytes 2097152 | tf_op jit(solution)/shard_map/all_to_all | solution.py:533
  27.7 106.1 %all-gather.7.cloned.1.call-start = ((), (), s32[]{:S(2)}) async-start(), calls=%async_computation.15 | async-start | bytes 1179648 | tf_op jit(solution)/shard_map/all_gather | solution.py:596
  28.5 18.5 %collective-permute-start.3 = (bf16[10,1,512]{2,1,0:T(2,128)(2,1)S(1)}, bf16[10,1,512]{2,1,0:T(2,128)(2,1)S(1)}, u32[]{:S(2)}, u32[]{:S(2)}) collective-permute-start(bf16[10,1,512]{2,1,0:T(2,128)(2,1)S(1)} %get-tuple-element.102), channel_id=1, source_target_pairs={{1,0},{2,1},{3,2},{4,3},{5,4},{6,5},{7,6},{0,7},{9,8},{10,9},{11,1... | collective-permute-start | bytes 30728 | tf_op jit(solution)/shard_map/ppermute | solution.py:568
  33.5 13.5 %collective-permute-start.2 = (bf16[10,1,512]{2,1,0:T(2,128)(2,1)S(1)}, bf16[10,1,512]{2,1,0:T(2,128)(2,1)S(1)}, u32[]{:S(2)}, u32[]{:S(2)}) collective-permute-start(bf16[10,1,512]{2,1,0:T(2,128)(2,1)S(1)} %get-tuple-element.101), channel_id=1, source_target_pairs={{0,1},{1,2},{2,3},{3,4},{4,5},{5,6},{6,7},{7,0},{8,9},{9,10},{10,1... | collective-permute-start | bytes 30728 | tf_op jit(solution)/shard_map/ppermute | solution.py:567
  59.5 19.2 %all-to-all-start.3 = ((bf16[8,36,1024]{2,1,0:T(8,128)(2,1)}), bf16[8,36,1024]{2,1,0:T(8,128)(2,1)S(1)}, u32[]{:S(2)}, u32[]{:S(2)}) async-start(bf16[8,36,1024]{2,1,0:T(8,128)(2,1)} %get-tuple-element.43), calls=%async_computation.3 | async-start | bytes 1310720 | tf_op jit(solution)/shard_map/all_to_all | solution.py:533
  78.7 24.8 %all-to-all-start.1 = ((bf16[16,36,1024]{2,1,0:T(8,128)(2,1)}), bf16[16,36,1024]{2,1,0:T(8,128)(2,1)S(1)}, u32[]{:S(2)}, u32[]{:S(2)}) async-start(bf16[16,36,1024]{2,1,0:T(8,128)(2,1)} %get-tuple-element.40), calls=%async_computation.1 | async-start | bytes 2621440 | tf_op jit(solution)/shard_map/all_to_all | solution.py:533
  82.7 55.5 %all-gather.5.cloned.1.call-start = ((), (), s32[]{:S(2)}) async-start(), calls=%async_computation.14 | async-start | bytes 1114112 | tf_op jit(solution)/shard_map/all_gather | solution.py:595
  103.5 13.0 %all-to-all-start.4 = ((bf16[8,32,1024]{2,1,0:T(8,128)(2,1)}), bf16[8,32,1024]{2,1,0:T(8,128)(2,1)S(1)}, u32[]{:S(2)}, u32[]{:S(2)}) async-start(bf16[8,32,1024]{2,1,0:T(8,128)(2,1)} %close_col.2), calls=%async_computation.4 | async-start | bytes 1048576 | tf_op jit(solution)/shard_map/all_to_all | solution.py:533
  117.4 24.7 %all-to-all-start.2 = ((bf16[16,32,1024]{2,1,0:T(8,128)(2,1)}), bf16[16,32,1024]{2,1,0:T(8,128)(2,1)S(1)}, u32[]{:S(2)}, u32[]{:S(2)}) async-start(bf16[16,32,1024]{2,1,0:T(8,128)(2,1)} %close_row.2), calls=%async_computation.2 | async-start | bytes 2097152 | tf_op jit(solution)/shard_map/all_to_all | solution.py:533
  166.8 14.1 %all-to-all-start.7 = ((bf16[8,32,1024]{2,1,0:T(8,128)(2,1)}), bf16[8,32,1024]{2,1,0:T(8,128)(2,1)S(1)}, u32[]{:S(2)}, u32[]{:S(2)}) async-start(bf16[8,32,1024]{2,1,0:T(8,128)(2,1)} %back_sums_across.1), calls=%async_computation.7 | async-start | bytes 1048576 | tf_op jit(solution)/shard_map/all_to_all | solution.py:533
  180.9 24.5 %all-to-all-start.5 = ((bf16[16,32,1024]{2,1,0:T(8,128)(2,1)}), bf16[16,32,1024]{2,1,0:T(8,128)(2,1)S(1)}, u32[]{:S(2)}, u32[]{:S(2)}) async-start(bf16[16,32,1024]{2,1,0:T(8,128)(2,1)} %back_sums_down.1), calls=%async_computation.5 | async-start | bytes 2097152 | tf_op jit(solution)/shard_map/all_to_all | solution.py:533
  205.4 13.0 %all-to-all-start.8 = ((bf16[8,32,1024]{2,1,0:T(8,128)(2,1)}), bf16[8,32,1024]{2,1,0:T(8,128)(2,1)S(1)}, u32[]{:S(2)}, u32[]{:S(2)}) async-start(bf16[8,32,1024]{2,1,0:T(8,128)(2,1)} %close_col.3), calls=%async_computation.8 | async-start | bytes 1048576 | tf_op jit(solution)/shard_map/all_to_all | solution.py:533
  218.3 21.6 %all-to-all-start.6 = ((bf16[16,32,1024]{2,1,0:T(8,128)(2,1)}), bf16[16,32,1024]{2,1,0:T(8,128)(2,1)S(1)}, u32[]{:S(2)}, u32[]{:S(2)}) async-start(bf16[16,32,1024]{2,1,0:T(8,128)(2,1)} %close_row.3), calls=%async_computation.6 | async-start | bytes 2097152 | tf_op jit(solution)/shard_map/all_to_all | solution.py:533
  239.9 28.1 %all-to-all-start.9 = ((bf16[128,8,512]{2,1,0:T(8,128)(2,1)}), bf16[128,8,512]{2,1,0:T(8,128)(2,1)}, u32[]{:S(2)}, u32[]{:S(2)}) async-start(bf16[128,8,512]{2,1,0:T(8,128)(2,1)} %bitcast.122), calls=%async_computation.9 | async-start | bytes 2097152 | tf_op jit(solution)/shard_map/all_to_all | solution.py:556
  269.4 33.7 %all-to-all-start.10 = ((bf16[128,8,512]{2,1,0:T(8,128)(2,1)}), bf16[128,8,512]{2,1,0:T(8,128)(2,1)S(1)}, u32[]{:S(2)}, u32[]{:S(2)}) async-start(bf16[128,8,512]{2,1,0:T(8,128)(2,1)} %bitcast.33), calls=%async_computation.10 | async-start | bytes 2097152 | tf_op jit(solution)/shard_map/all_to_all | solution.py:556
  307.6 6.1 %collective-permute-start.6 = (bf16[1,16,1024]{2,1,0:T(8,128)(2,1)S(1)}, bf16[1,16,1024]{2,1,0:T(8,128)(2,1)S(1)}, u32[]{:S(2)}, u32[]{:S(2)}) collective-permute-start(bf16[1,16,1024]{2,1,0:T(8,128)(2,1)S(1)} %get-tuple-element.92), channel_id=1, source_target_pairs={{8,0},{16,8},{24,16},{32,24},{40,32},{48,40},{56,48},{64,56},{72,6... | collective-permute-start | bytes 98312 | tf_op jit(solution)/shard_map/ppermute | solution.py:568
  312.0 7.0 %collective-permute-start.5 = (bf16[1,16,1024]{2,1,0:T(8,128)(2,1)S(1)}, bf16[1,16,1024]{2,1,0:T(8,128)(2,1)S(1)}, u32[]{:S(2)}, u32[]{:S(2)}) collective-permute-start(bf16[1,16,1024]{2,1,0:T(8,128)(2,1)S(1)} %get-tuple-element.91), channel_id=1, source_target_pairs={{0,8},{8,16},{16,24},{24,32},{32,40},{40,48},{48,56},{56,64},{64,7... | collective-permute-start | bytes 98312 | tf_op jit(solution)/shard_map/ppermute | solution.py:567
  319.0 5.2 %collective-permute-start.7 = (bf16[10,1,1024]{2,1,0:T(2,128)(2,1)S(1)}, bf16[10,1,1024]{2,1,0:T(2,128)(2,1)S(1)}, u32[]{:S(2)}, u32[]{:S(2)}) collective-permute-start(bf16[10,1,1024]{2,1,0:T(2,128)(2,1)S(1)} %get-tuple-element.86), channel_id=1, source_target_pairs={{1,0},{2,1},{3,2},{4,3},{5,4},{6,5},{7,6},{0,7},{9,8},{10,9},{11,1... | collective-permute-start | bytes 61448 | tf_op jit(solution)/shard_map/ppermute | solution.py:568
  322.6 6.1 %collective-permute-start.8 = (bf16[10,1,1024]{2,1,0:T(2,128)(2,1)S(1)}, bf16[10,1,1024]{2,1,0:T(2,128)(2,1)S(1)}, u32[]{:S(2)}, u32[]{:S(2)}) collective-permute-start(bf16[10,1,1024]{2,1,0:T(2,128)(2,1)S(1)} %get-tuple-element.87), channel_id=1, source_target_pairs={{0,1},{1,2},{2,3},{3,4},{4,5},{5,6},{6,7},{7,0},{8,9},{9,10},{10,1... | collective-permute-start | bytes 61448 | tf_op jit(solution)/shard_map/ppermute | solution.py:567
  331.0 24.2 %all-to-all-start.11 = ((bf16[128,8,512]{2,1,0:T(8,128)(2,1)}), bf16[128,8,512]{2,1,0:T(8,128)(2,1)}, u32[]{:S(2)}, u32[]{:S(2)}) async-start(bf16[128,8,512]{2,1,0:T(8,128)(2,1)} %bitcast.42), calls=%async_computation.11 | async-start | bytes 2097152 | tf_op jit(solution)/shard_map/all_to_all | solution.py:556
  336.8 28.1 %copy-start.7 = (bf16[1024,512]{1,0:T(8,128)(2,1)S(1)}, bf16[1024,512]{1,0:T(8,128)(2,1)}, u32[]{:S(2)}) copy-start(bf16[1024,512]{1,0:T(8,128)(2,1)} %all-gather.7.cloned.1.call-done) | copy-start | bytes 3145732
  355.9 13.0 %all-to-all-start.13 = ((f32[16,8,512]{2,1,0:T(8,128)}), f32[16,8,512]{2,1,0:T(8,128)S(1)}, u32[]{:S(2)}, u32[]{:S(2)}) async-start(f32[16,8,512]{2,1,0:T(8,128)} %broadcast_in_dim.11), calls=%async_computation.13 | async-start | bytes 524288 | tf_op jit(solution)/shard_map/all_to_all | solution.py:533
  361.6 5.2 %collective-permute-start.9 = (bf16[8,512]{1,0:T(8,128)(2,1)S(1)}, bf16[8,512]{1,0:T(8,128)(2,1)S(1)}, u32[]{:S(2)}, u32[]{:S(2)}) collective-permute-start(bf16[8,512]{1,0:T(8,128)(2,1)S(1)} %get-tuple-element.116), channel_id=1, source_target_pairs={{0,64},{8,72},{16,80},{24,88},{32,96},{40,104},{48,112},{56,120},{... | collective-permute-start | bytes 24584 | tf_op jit(solution)/shard_map/ppermute | solution.py:543
  369.6 9.9 %all-to-all-start.12 = ((bf16[8,2,8,512]{3,2,1,0:T(8,128)(2,1)}), bf16[8,2,8,512]{3,2,1,0:T(8,128)(2,1)S(1)}, u32[]{:S(2)}, u32[]{:S(2)}) async-start(bf16[8,2,8,512]{3,2,1,0:T(8,128)(2,1)} %broadcast_in_dim.10), calls=%async_computation.12 | async-start | bytes 262144 | tf_op jit(solution)/shard_map/all_to_all | solution.py:533
  (34 other events, 456.7 us)
Sparse Core Ops, SparseCore 0:
  47.1 38.6 all-gather.6
  88.8 49.2 all-gather.4
where the time goes:
time: 392 us; the launch traced here: 388 us
  waiting for transfers between devices  117 us (30%)
  Pallas kernels  117 us (30%)
  starting transfers between devices  92.7 us (24%)
  local copies, waits for them, and re-layouts  19.1 us (5%)
  between operations  14.9 us (4%)
  matrix products  14 us (4%)
  other arithmetic  13.2 us (3%)
    pallas_call x8, Pallas kernels, call(): pl.pallas_call(kernel, grid=(TILES,), in_specs=specs, out_specs=[spec for...  102 us
    all_to_all x11, waiting for transfers between devices, swapped(): return lax.all_to_all(x, axis, 0, 0, tiled=True)  84.8 us
    all_to_all x11, starting transfers between devices, swapped(): return lax.all_to_all(x, axis, 0, 0, tiled=True)  46.1 us
    all_to_all x3, starting transfers between devices, reduced(): lax.all_to_all(pieces.reshape(128, 8, C), ('row', 'col'), 0, 0, tiled=True)  21.3 us
    ppermute x4, starting transfers between devices, with_halo(): lax.ppermute(head, axis, [((i + 1) % count, i) for i in range(count)])  18.4 us
    all_to_all x3, waiting for transfers between devices, reduced(): lax.all_to_all(pieces.reshape(128, 8, C), ('row', 'col'), 0, 0, tiled=True)  15.8 us
    pallas_call x4, Pallas kernels, closed(): pl.pallas_call(partial(close_kernel, peers=peers, flip=flip), grid=(E //...  11 us
    ppermute x4, waiting for transfers between devices, with_halo(): lax.ppermute(tail_part, axis, [(i, (i + 1) % count) for i in range(count)])  9.74 us
  transfers between devices with their start and end apart: 26, of which 17 were waited for; matrix products, arithmetic and copies ran while one was open for 8% of the time, Pallas kernels for 24%

commit v1 on v0

--- a/solution.py
+++ b/solution.py
@@ -7,11 +7,11 @@
 from jax.experimental.pallas import tpu as pltpu
 from jax.sharding import PartitionSpec as P
 
+
 C = 512
 E = 1024
 N = 16
 R = 32
-K = 4
 ROWS = 8
 COLS = 16
 CELLS = ROWS * COLS
@@ -270,7 +270,6 @@
             def backward(p, pulls):
                 rows = at_slab(first + p)
                 before = at_slab(first + at + p)
-                after = at_slab(first + at + p + 1)
                 st = step_ref[d, rows, :]
                 u = us_ref[rows, :]
                 dy = dys_ref[rows, :]
@@ -278,7 +277,6 @@
                 back_step = []
                 new = []
                 for n in range(N):
-                    acc_ref[d, N + n, rows, :] += hs_ref[d, n, after, :] * dy
                     g = pulls[n] + dy * tab_ref[d, N + n, rows, :]
                     acc_ref[d, n, rows, :] += g * u
                     back_u.append(g * tab_ref[d, n, rows, :])
@@ -310,18 +308,52 @@
     def _():
         for d in range(2):
             total = rank_ref[d]
-            ones = jnp.ones((2 * LANES, LANES), BF16)
-            column = lax.broadcasted_iota(jnp.int32, (CELLS, LANES), 1)
-            for j in range(2 * N):
-                lane = d * (R + 2 * N) + R + j
-                both = jnp.concatenate(split(acc_ref[d, j]), axis=1)
-                row_sums = jnp.dot(both, ones, preferred_element_type=F32)
-                total = jnp.where(column == lane, row_sums, total)
+            for n in range(N):
+                total = with_row_sums(total, acc_ref[d, n], d * (R + 2 * N) + R + n)
             rank_ref[d] = total
-            for t in range(SLABS):
-                rows = slab_rows(down, d, t)
-                piece = rank_ref[d, t * 8 : t * 8 + 8, :]
-                pg_ref[rows, :] = pg_ref[rows, :] + piece if d else piece
+            from_slabs(down, d, rank_ref, pg_ref)
+
+
+def with_row_sums(total, values, lane):
+    ones = jnp.ones((2 * LANES, LANES), BF16)
+    column = lax.broadcasted_iota(jnp.int32, (CELLS, LANES), 1)
+    sums = jnp.dot(jnp.concatenate(split(values), axis=1), ones, preferred_element_type=F32)
+    return jnp.where(column == lane, sums, total)
+
+
+def from_slabs(down, d, src_ref, out_ref):
+    for t in range(SLABS):
+        rows = slab_rows(down, d, t)
+        piece = src_ref[d, t * 8 : t * 8 + 8, :]
+        out_ref[rows, :] = out_ref[rows, :] + piece if d else piece
+
+
+def out_grads_kernel(dy_ref, hs_ref, pg_ref, dys_ref, acc_ref, total_ref, *, down):
+    n = pl.program_id(0)
+
+    @pl.when(n == 0)
+    def _():
+        for i in range(TILES):
+            acc_ref[...] = dy_ref[:, i * LANES : (i + 1) * LANES]
+            for d in range(2):
+                for t in range(SLABS):
+                    dys_ref[d, i, t * 8 : t * 8 + 8, :] = acc_ref[slab_rows(down, d, t), :]
+        total_ref[...] = jnp.zeros(total_ref.shape, F32)
+
+    for d in range(2):
+        for at, (first, length, _) in enumerate(chains(down)):
+            for p in range(length):
+                rows = at_slab(first + p)
+                after = at_slab(first + at + p + 1)
+                acc_ref[rows, :] = tree_sum(
+                    [hs_ref[i, d, after, :] * dys_ref[d, i, rows, :] for i in range(TILES)]
+                )
+        total_ref[d] = with_row_sums(total_ref[d], acc_ref[...], d * (R + 2 * N) + R + N + n)
+
+    @pl.when(n == N - 1)
+    def _():
+        for d in range(2):
+            from_slabs(down, d, total_ref, pg_ref)
 
 
 def close_kernel(info_ref, ends_ref, rate_ref, out_ref, *, peers, flip):
@@ -399,7 +431,7 @@
 PARAMS = pltpu.CompilerParams(dimension_semantics=("arbitrary",), vmem_limit_bytes=56 * 1024 * 1024)
 
 
-def call(kernel, name, specs, outs, scratch, args):
+def call(kernel, specs, outs, scratch, args):
     return pl.pallas_call(
         kernel,
         grid=(TILES,),
@@ -408,7 +440,6 @@
         out_shape=[jax.ShapeDtypeStruct(shape, dtype) for _, (shape, dtype) in outs],
         scratch_shapes=scratch,
         compiler_params=PARAMS,
-        name=name,
     )(*args)
 
 
@@ -416,7 +447,6 @@
     lines = COLS if down else ROWS
     return call(
         partial(sums_kernel, down=down),
-        "sums_down" if down else "sums_across",
         [tiled((CELLS,)), whole((CELLS, LANES)), tiled((2, LANES)), tiled((2,)), tiled((2, N))],
         [
             (tiled((lines, 2 * N + 4)), ((lines, 2 * N + 4, E), BF16)),
@@ -439,7 +469,6 @@
     lines = COLS if down else ROWS
     return call(
         partial(outputs_kernel, down=down),
-        "outputs_down" if down else "outputs_across",
         [
             tiled((CELLS,)), whole((CELLS, LANES)), by_tile(PAIR), tiled((2, N)), tiled((1,)),
             tiled((lines, 2 * N)),
@@ -460,7 +489,6 @@
     lines = COLS if down else ROWS
     return call(
         partial(back_sums_kernel, down=down),
-        "back_sums_down" if down else "back_sums_across",
         [tiled((CELLS,)), whole((CELLS, LANES)), by_tile(PAIR), tiled((2, N))],
         [(tiled((lines, 2 * N)), ((lines, 2 * N, E), BF16))],
         [
@@ -476,7 +504,6 @@
     cells = vmem(CELLS, LANES)
     return call(
         partial(grads_kernel, down=down),
-        "grads_down" if down else "grads_across",
         [
             tiled((CELLS,)), tiled((CELLS,)), whole((CELLS, LANES)), by_tile(PAIR), by_tile(PAIR),
             tiled((2, N)), tiled((1,)), tiled((2, LANES)),
@@ -487,17 +514,37 @@
             (whole((CELLS, LANES)), ((CELLS, LANES), F32)),
         ],
         [
-            vmem(2, CELLS, LANES), vmem(2, 2 * N, CELLS, LANES), vmem(2, 2 * N, CELLS, LANES),
+            vmem(2, CELLS, LANES), vmem(2, 2 * N, CELLS, LANES), vmem(2, N, CELLS, LANES),
             vmem(2, CELLS, LANES), cells, cells, cells, cells, cells, cells,
             vmem(N, 8, LANES), vmem(8 * N, LANES),
         ],
         (active, back, proj, steps, sigs, rates, skip, dtw, kept, tails),
     )
+
+
+def block_out_grads(down, back, kept):
+    rows = kept_rows(down)
+    return pl.pallas_call(
+        partial(out_grads_kernel, down=down),
+        grid=(N,),
+        in_specs=[
+            whole((CELLS, E)),
+            pl.BlockSpec((TILES, 2, None, rows, LANES), lambda n: (0, 0, n, 0, 0)),
+        ],
+        out_specs=whole((CELLS, LANES)),
+        out_shape=jax.ShapeDtypeStruct((CELLS, LANES), F32),
+        scratch_shapes=[
+            vmem(2, TILES, CELLS, LANES), vmem(CELLS, LANES), vmem(2, CELLS, LANES),
+        ],
+        compiler_params=PARAMS,
+        name="out_grads_down" if down else "out_grads_across",
+    )(back, kept)
 
 
 def closed(axis, info, ends, rates, flip):
     peers = lax.axis_size(axis)
     lines = info.shape[0]
+
     def wide(*lead):
         return pl.BlockSpec((*lead, WIDE), lambda i: (*(0,) * len(lead), i))
 
@@ -508,7 +555,6 @@
         out_specs=wide(lines, 2 * N),
         out_shape=jax.ShapeDtypeStruct((lines, 2 * N, E), BF16),
         compiler_params=PARAMS,
-        name="close_" + axis,
     )(info, ends, rates)
 
 
@@ -529,13 +575,13 @@
     )(y0, y1, gate, gain, back)
 
 
-def swapped(x, axis):
+def swap(x, axis):
     return lax.all_to_all(x, axis, 0, 0, tiled=True)
 
 
 def sent_to_all(shard, axis):
     peers = lax.axis_size(axis)
-    return swapped(jnp.broadcast_to(shard[None], (peers, *shard.shape)), axis)
+    return swap(jnp.broadcast_to(shard[None], (peers, *shard.shape)), axis)
 
 
 def across(shard):
@@ -552,8 +598,8 @@
     return part.astype(BF16).reshape(8, 2, 8, 8, C).transpose(1, 0, 2, 3, 4)
 
 
-def reduced(pieces):
-    pieces = lax.all_to_all(pieces.reshape(128, 8, C), ("row", "col"), 0, 0, tiled=True)
+def reduced(pieces, rows):
+    pieces = lax.all_to_all(pieces.reshape(128, rows, C), ("row", "col"), 0, 0, tiled=True)
     return jnp.sum(pieces.astype(F32), axis=0)
 
 
@@ -572,7 +618,7 @@
     return cells
 
 
-def local(
+def block(
     field,
     in_weight,
     conv_weight,
@@ -586,14 +632,14 @@
     grad_out,
 ):
     upper = lax.axis_index("row") >= lax.axis_size("row") // 2
+    out_full = lax.all_gather(out_weight, "col").reshape(E, C)
     first, last = in_weight[: C // 2], in_weight[C // 2 :]
     other = across(jnp.where(upper, first, last))
     in_source = sent_to_all(jnp.where(upper, other, first), "row")
     in_gate = jnp.where(upper, last, other)
-    in_source, in_gate, out_weight = lax.optimization_barrier((in_source, in_gate, out_weight))
+    in_source, in_gate = lax.optimization_barrier((in_source, in_gate))
     in_source = from_halves(in_source)
     in_gate = from_halves(lax.all_gather(in_gate, "row"))
-    out_full = lax.all_gather(out_weight, "col").reshape(E, C)
     field_rows = field.reshape(CELLS, C)
     grad_rows = grad_out.reshape(CELLS, C)
     field_wide = with_halo(field, (("row", 0), ("col", 1)), 1)
@@ -633,9 +679,9 @@
         block_sums(down, active, projs[i], pads[i], dt_bias[k : k + 2], rates[i])
         for i, (down, _, k) in enumerate(kinds)
     ]
-    infos = [swapped(sums[i][0], axis) for i, (_, axis, _) in enumerate(kinds)]
+    infos = [swap(sums[i][0], axis) for i, (_, axis, _) in enumerate(kinds)]
     starts = [
-        swapped(closed(axis, infos[i], infos[i], rates[i], False), axis)
+        swap(closed(axis, infos[i], infos[i], rates[i], False), axis)
         for i, (_, axis, _) in enumerate(kinds)
     ]
     outs = [
@@ -654,32 +700,37 @@
     )
 
     back_ends = [
-        swapped(block_back_sums(down, back_summed, projs[i], sums[i][1], rates[i]), axis)
+        swap(block_back_sums(down, back_summed, projs[i], sums[i][1], rates[i]), axis)
         for i, (down, axis, _) in enumerate(kinds)
     ]
+    pieces = jnp.concatenate(
+        [
+            out_part.astype(BF16).reshape(8, 16, 8, C).transpose(1, 0, 2, 3).reshape(128, 8, C),
+            owner_order(gate_part).reshape(128, 8, C),
+        ],
+        axis=1,
+    )
+    out_grads = [
+        block_out_grads(down, back_summed, outs[i][1]) for i, (down, _, _) in enumerate(kinds)
+    ]
     tails = [
-        swapped(closed(axis, infos[i], back_ends[i], rates[i], True), axis)
+        swap(closed(axis, infos[i], back_ends[i], rates[i], True), axis)
         for i, (_, axis, _) in enumerate(kinds)
     ]
-    out_pieces = out_part.astype(BF16).reshape(8, 16, 8, C).transpose(1, 0, 2, 3)
-    out_pieces, tails = lax.optimization_barrier((out_pieces, tails))
-    out_piece = reduced(out_pieces)
-    grads_of = [
-        partial(
-            block_grads, down, active, back_summed, projs[i], sums[i][1], sums[i][2], rates[i],
-            skips[i], pads[i], outs[i][1],
+    pieces, tails = lax.optimization_barrier((pieces, tails))
+    done_piece = reduced(pieces, 16)
+    grads = [
+        block_grads(
+            down, active, back_summed, projs[i], sums[i][1], sums[i][2], rates[i], skips[i],
+            pads[i], outs[i][1], tails[i],
         )
         for i, (down, _, _) in enumerate(kinds)
     ]
-    grads = [grads_of[0](tails[0])]
-    out_piece, gate_pieces, grads[0], tails[1] = lax.optimization_barrier(
-        (out_piece, owner_order(gate_part), grads[0], tails[1])
-    )
-    gate_piece = reduced(gate_pieces)
-    grads.append(grads_of[1](tails[1]))
-    out_piece, gate_piece, grads = lax.optimization_barrier((out_piece, gate_piece, grads))
-    grad_out_weight = sent_to_all(out_piece, "row").reshape(E // 8, C)
-    proj_grads = jnp.concatenate([grads[0][1], grads[1][1]], axis=1)
+    done_piece, grads = lax.optimization_barrier((done_piece, grads))
+    grad_out_weight = lax.all_gather(jnp.pad(done_piece[:8], ((0, 56), (0, 0))), "row")
+    grad_out_weight = grad_out_weight[:, :8].reshape(E // 8, C)
+    gate_piece = done_piece[8:]
+    proj_grads = jnp.concatenate([grads[i][1] + out_grads[i] for i in range(2)], axis=1)
     high, low = split(proj_grads)
     dims = (((1,), (1,)), ((), ()))
     back_active = (
@@ -701,7 +752,7 @@
     source_part = lax.dot_general(
         back_source, field_rows, (((0,), (0,)), ((), ())), preferred_element_type=F32
     )
-    source_piece = reduced(owner_order(source_part))
+    source_piece = reduced(owner_order(source_part).reshape(128, 8, C), 8)
     dims = (((1,), (1,)), ((), ()))
     grad_field = (
         grad_rows.astype(F32)
@@ -737,4 +788,4 @@
         P("row", "col", None),
     )
     out_specs = (P("row", "col", None), P("row", "col", None), P(None, "row"), P("col", None))
-    return jax.shard_map(local, mesh=mesh, in_specs=in_specs, out_specs=out_specs, check_vma=False)
+    return jax.shard_map(block, mesh=mesh, in_specs=in_specs, out_specs=out_specs, check_vma=False)

time: 392 us -> 398 us (1.015)
  Pallas kernels: 117 us -> 136 us
  starting transfers between devices: 92.7 us -> 76 us
  waiting for transfers between devices: 117 us -> 122 us
    pallas_call x0 -> x2, Pallas kernels: none -> 27.6 us  [block_out_grads(): pl.pallas_call(partial(out_grads_kernel, down=down), grid=(N,), in_specs=...]
    all_to_all x14 -> x12, starting transfers between devices: 67.4 us -> 56 us  [the longest x10 43.2 us: swap(): return lax.all_to_all(x, axis, 0, 0, tiled=True)]
    pallas_call x8, Pallas kernels: 102 us -> 93.5 us  [call(): pl.pallas_call(kernel, grid=(TILES,), in_specs=specs, out_specs=[spec for...]
    all_to_all x14 -> x12, waiting for transfers between devices: 101 us -> 108 us  [the longest x10 86.2 us: swap(): return lax.all_to_all(x, axis, 0, 0, tiled=True)]
    ppermute x2, starting transfers between devices: 6.74 us -> 1.28 us  [across(): lax.ppermute(shard, 'row', [(i, (i + rows // 2) % rows) for i in range(ro...]
    ppermute x2, waiting for transfers between devices: 0.88 us -> 5.25 us  [across(): lax.ppermute(shard, 'row', [(i, (i + rows // 2) % rows) for i in range(ro...]
  transfers between devices with their start and end apart: 26 -> 25, of which waited for: 17 -> 15; matrix products, arithmetic and copies ran while one was open for 8% -> 9% of each run, Pallas kernels for 24% -> 29%
where the time goes in v1:
time: 398 us; the launch traced here: 394 us
  Pallas kernels  136 us (34%)
  waiting for transfers between devices  122 us (31%)
  starting transfers between devices  76 us (19%)
  local copies, waits for them, and re-layouts  17.4 us (4%)
  other arithmetic  14.6 us (4%)
  between operations  14.5 us (4%)
  matrix products  13 us (3%)
    pallas_call x8, Pallas kernels, call(): pl.pallas_call(kernel, grid=(TILES,), in_specs=specs, out_specs=[spec for...  93.5 us
    all_to_all x10, waiting for transfers between devices, swap(): return lax.all_to_all(x, axis, 0, 0, tiled=True)  86.2 us
    all_to_all x10, starting transfers between devices, swap(): return lax.all_to_all(x, axis, 0, 0, tiled=True)  43.2 us
    pallas_call x2, Pallas kernels, block_out_grads(): pl.pallas_call(partial(out_grads_kernel, down=down), grid=(N,), in_specs=...  27.6 us
    all_to_all x2, waiting for transfers between devices, reduced(): lax.all_to_all(pieces.reshape(128, rows, C), ('row', 'col'), 0, 0, tiled=...  21.5 us
    ppermute x4, starting transfers between devices, with_halo(): lax.ppermute(head, axis, [((i + 1) % count, i) for i in range(count)])  16.3 us
    all_to_all x2, starting transfers between devices, reduced(): lax.all_to_all(pieces.reshape(128, rows, C), ('row', 'col'), 0, 0, tiled=...  12.8 us
    pallas_call x4, Pallas kernels, closed(): pl.pallas_call(partial(close_kernel, peers=peers, flip=flip), grid=(E //...  11.2 us
  transfers between devices with their start and end apart: 25, of which 15 were waited for; matrix products, arithmetic and copies ran while one was open for 9% of the time, Pallas kernels for 29%

profile of v1, /device:TPU:0, one launch (start us, length us, event | category | flops | bytes accessed | tf_op | source)
XLA Modules:
  0.0 393.9 jit_solution(18432340198865472223)
XLA Ops:
  8.7 5.0 %collective-permute-start.1 = (bf16[1,16,512]{2,1,0:T(8,128)(2,1)S(1)}, bf16[1,16,512]{2,1,0:T(8,128)(2,1)S(1)}, u32[]{:S(2)}, u32[]{:S(2)}) collective-permute-start(bf16[1,16,512]{2,1,0:T(8,128)(2,1)S(1)} %get-tuple-element.91), channel_id=1, source_target_pairs={{8,0},{16,8},{24,16},{32,24},{40,32},{48,40},{56,48},{64,56},{72,6... | collective-permute-start | bytes 49160 | tf_op jit(solution)/shard_map/ppermute | solution.py:614
  23.2 5.5 %all-to-all-start = ((bf16[16,256,128]{2,1,0:T(8,128)(2,1)}), bf16[16,256,128]{2,1,0:T(8,128)(2,1)S(1)}, u32[]{:S(2)}, u32[]{:S(2)}) async-start(bf16[16,256,128]{2,1,0:T(8,128)(2,1)} %broadcast_in_dim.6), calls=%async_computation | async-start | bytes 2097152 | tf_op jit(solution)/shard_map/all_to_all | solution.py:579
  34.5 18.0 %all-to-all-done = bf16[16,256,128]{2,1,0:T(8,128)(2,1)S(1)} async-done(((bf16[16,256,128]{2,1,0:T(8,128)(2,1)}), bf16[16,256,128]{2,1,0:T(8,128)(2,1)S(1)}, u32[]{:S(2)}, u32[]{:S(2)}) %all-to-all-start) | async-done | bytes 1048608 | tf_op jit(solution)/shard_map/all_to_all | solution.py:579
  56.8 9.4 %shard_map.141 = (bf16[8,36,1024]{2,1,0:T(8,128)(2,1)}, f32[8,2,128,128]{3,2,1,0:T(8,128)}, f32[8,2,128,128]{3,2,1,0:T(8,128)}) custom-call(bf16[128,1024]{1,0:T(8,128)(2,1)} %copy-done.2, f32[128,128]{1,0:T(8,128)} %get-tuple-element.89.proj_ref, bf16[2,128,1024]{2,1,0:T(8,128)(2,1)} %pad_maximum_fusion.5.dtw_ref, f32[2,1024]{1,0:T(2,128)} %get-tuple-element.106.bias_ref, ...), custom_call_target="tpu_custom_call" | custom-call | tf_op jit(solution)/shard_map/pallas_call | solution.py:435
  66.1 4.1 %all-to-all-start.3 = ((bf16[8,36,1024]{2,1,0:T(8,128)(2,1)}), bf16[8,36,1024]{2,1,0:T(8,128)(2,1)S(1)}, u32[]{:S(2)}, u32[]{:S(2)}) async-start(bf16[8,36,1024]{2,1,0:T(8,128)(2,1)} %get-tuple-element.36), calls=%async_computation.3 | async-start | bytes 1310720 | tf_op jit(solution)/shard_map/all_to_all | solution.py:579
  71.1 8.9 %shard_map.138 = (bf16[16,36,1024]{2,1,0:T(8,128)(2,1)}, f32[8,2,128,128]{3,2,1,0:T(8,128)}, f32[8,2,128,128]{3,2,1,0:T(8,128)}) custom-call(bf16[128,1024]{1,0:T(8,128)(2,1)} %copy-done.2, f32[128,128]{1,0:T(8,128)} %get-tuple-element.90.proj_ref, bf16[2,128,1024]{2,1,0:T(8,128)(2,1)} %pad_maximum_fusion.4.dtw_ref, f32[2,1024]{1,0:T(2,128)} %get-tuple-element.107.bias_ref, ...), custom_call_target="tpu_custom_call" | custom-call | tf_op jit(solution)/shard_map/pallas_call | solution.py:435
  80.6 3.8 all-to-all-start.1
  87.5 17.8 %all-to-all-done.1.info_ref.ends_ref = bf16[16,36,1024]{2,1,0:T(8,128)(2,1)S(1)} async-done(((bf16[16,36,1024]{2,1,0:T(8,128)(2,1)}), bf16[16,36,1024]{2,1,0:T(8,128)(2,1)S(1)}, u32[]{:S(2)}, u32[]{:S(2)}) %all-to-all-start.1) | async-done | bytes 1179680 | tf_op jit(solution)/shard_map/all_to_all | solution.py:579
  105.3 5.0 %all-to-all-start.4 = ((bf16[8,32,1024]{2,1,0:T(8,128)(2,1)}), bf16[8,32,1024]{2,1,0:T(8,128)(2,1)S(1)}, u32[]{:S(2)}, u32[]{:S(2)}) async-start(bf16[8,32,1024]{2,1,0:T(8,128)(2,1)} %shard_map.142), calls=%async_computation.4 | async-start | bytes 1048576 | tf_op jit(solution)/shard_map/all_to_all | solution.py:579
  113.6 6.0 %all-to-all-done.4.start_ref = bf16[8,32,1024]{2,1,0:T(8,128)(2,1)S(1)} async-done(((bf16[8,32,1024]{2,1,0:T(8,128)(2,1)}), bf16[8,32,1024]{2,1,0:T(8,128)(2,1)S(1)}, u32[]{:S(2)}, u32[]{:S(2)}) %all-to-all-start.4) | async-done | bytes 524320 | tf_op jit(solution)/shard_map/all_to_all | solution.py:579
  120.4 3.8 all-to-all-start.2
  127.3 11.9 %shard_map.143 = (f32[128,1024]{1,0:T(8,128)}, f32[8,2,16,136,128]{4,3,2,1,0:T(8,128)}) custom-call(bf16[128,1024]{1,0:T(8,128)(2,1)} %copy-done.2, f32[128,128]{1,0:T(8,128)} %get-tuple-element.89.proj_ref, f32[8,2,128,128]{3,2,1,0:T(8,128)} %get-tuple-element.35.step_ref, f32[2,16,1024]{2,1,0:T(8,128)} %get-tuple-element.79.rate_ref, ...), custom_call_target="tpu_custom_call" | custom-call | tf_op jit(solution)/shard_map/pallas_call | solution.py:435
  144.2 12.1 %shard_map.140 = (f32[128,1024]{1,0:T(8,128)}, f32[8,2,16,144,128]{4,3,2,1,0:T(8,128)}) custom-call(bf16[128,1024]{1,0:T(8,128)(2,1)} %copy-done.2, f32[128,128]{1,0:T(8,128)} %get-tuple-element.90.proj_ref, f32[8,2,128,128]{3,2,1,0:T(8,128)} %get-tuple-element.32.step_ref, f32[2,16,1024]{2,1,0:T(8,128)} %get-tuple-element.80.rate_ref, ...), custom_call_target="tpu_custom_call" | custom-call | tf_op jit(solution)/shard_map/pallas_call | solution.py:435
  156.3 4.1 %tail.1 = (bf16[128,1024]{1,0:T(8,128)(2,1)}, f32[128,1024]{1,0:T(8,128)}, bf16[128,1024]{1,0:T(8,128)(2,1)}) custom-call(f32[128,1024]{1,0:T(8,128)} %get-tuple-element.34.y0_ref, f32[128,1024]{1,0:T(8,128)} %get-tuple-element.37.y1_ref, bf16[128,1024]{1,0:T(8,128)(2,1)} %fusion.1.gate_ref, f32[1,1024]{1,0:T(1,128)} %bitcast.159, f32[128,1024]{1,0:T(8,128)} %fusion.43.back_ref), custom_call_target="tpu_custom_call" | custom-call | tf_op jit(solution)/shard_map/tail/pallas_call | solution.py:563
  160.3 7.6 %shard_map.146 = bf16[8,32,1024]{2,1,0:T(8,128)(2,1)} custom-call(f32[128,1024]{1,0:T(8,128)} %get-tuple-element.41.dy_ref, f32[128,128]{1,0:T(8,128)} %get-tuple-element.89.proj_ref, f32[8,2,128,128]{3,2,1,0:T(8,128)} %get-tuple-element.35.step_ref, f32[2,16,1024]{2,1,0:T(8,128)} %get-tuple-element.79.rate_ref), custom_call_target="tpu_custom_call" | custom-call | tf_op jit(solution)/shard_map/pallas_call | solution.py:435
  171.5 7.5 %shard_map.144 = bf16[16,32,1024]{2,1,0:T(8,128)(2,1)} custom-call(f32[128,1024]{1,0:T(8,128)} %get-tuple-element.41.dy_ref, f32[128,128]{1,0:T(8,128)} %get-tuple-element.90.proj_ref, f32[8,2,128,128]{3,2,1,0:T(8,128)} %get-tuple-element.32.step_ref, f32[2,16,1024]{2,1,0:T(8,128)} %get-tuple-element.80.rate_ref), custom_call_target="tpu_custom_call" | custom-call | tf_op jit(solution)/shard_map/pallas_call | solution.py:435
  181.4 7.0 %all-to-all-start.5 = ((bf16[16,32,1024]{2,1,0:T(8,128)(2,1)}), bf16[16,32,1024]{2,1,0:T(8,128)(2,1)S(1)}, u32[]{:S(2)}, u32[]{:S(2)}) async-start(bf16[16,32,1024]{2,1,0:T(8,128)(2,1)} %shard_map.144), calls=%async_computation.5 | async-start | bytes 2097152 | tf_op jit(solution)/shard_map/all_to_all | solution.py:579
  190.8 15.6 %all-to-all-done.5.ends_ref = bf16[16,32,1024]{2,1,0:T(8,128)(2,1)S(1)} async-done(((bf16[16,32,1024]{2,1,0:T(8,128)(2,1)}), bf16[16,32,1024]{2,1,0:T(8,128)(2,1)S(1)}, u32[]{:S(2)}, u32[]{:S(2)}) %all-to-all-start.5) | async-done | bytes 1048608 | tf_op jit(solution)/shard_map/all_to_all | solution.py:579
  213.1 6.3 %all-to-all-done.8.tail_ref = bf16[8,32,1024]{2,1,0:T(8,128)(2,1)S(1)} async-done(((bf16[8,32,1024]{2,1,0:T(8,128)(2,1)}), bf16[8,32,1024]{2,1,0:T(8,128)(2,1)S(1)}, u32[]{:S(2)}, u32[]{:S(2)}) %all-to-all-start.8) | async-done | bytes 524320 | tf_op jit(solution)/shard_map/all_to_all | solution.py:579
  219.4 3.7 all-to-all-start.6
  226.9 14.2 %all-to-all-done.6.tail_ref = bf16[16,32,1024]{2,1,0:T(8,128)(2,1)S(1)} async-done(((bf16[16,32,1024]{2,1,0:T(8,128)(2,1)}), bf16[16,32,1024]{2,1,0:T(8,128)(2,1)S(1)}, u32[]{:S(2)}, u32[]{:S(2)}) %all-to-all-start.6) | async-done | bytes 1048608 | tf_op jit(solution)/shard_map/all_to_all | solution.py:579
  242.0 5.8 %all-to-all-start.9 = ((bf16[128,16,512]{2,1,0:T(8,128)(2,1)}), bf16[128,16,512]{2,1,0:T(8,128)(2,1)}, u32[]{:S(2)}, u32[]{:S(2)}) async-start(bf16[128,16,512]{2,1,0:T(8,128)(2,1)} %pad_maximum_fusion), calls=%async_computation.9 | async-start | bytes 4194304 | tf_op jit(solution)/shard_map/all_to_all | solution.py:602
  248.0 13.8 %out_grads_across.1 = f32[128,128]{1,0:T(8,128)} custom-call(f32[128,1024]{1,0:T(8,128)} %get-tuple-element.41.dy_ref, f32[8,2,16,136,128]{4,3,2,1,0:T(8,128)} %get-tuple-element.49.hs_ref), custom_call_target="tpu_custom_call" | custom-call | tf_op jit(solution)/shard_map/out_grads_across/pallas_call | solution.py:527
  261.8 13.8 %out_grads_down.1 = f32[128,128]{1,0:T(8,128)} custom-call(f32[128,1024]{1,0:T(8,128)} %get-tuple-element.41.dy_ref, f32[8,2,16,144,128]{4,3,2,1,0:T(8,128)} %get-tuple-element.44.hs_ref), custom_call_target="tpu_custom_call" | custom-call | tf_op jit(solution)/shard_map/out_grads_down/pallas_call | solution.py:527
  275.7 19.0 %shard_map.149 = (f32[128,1024]{1,0:T(8,128)}, f32[128,128]{1,0:T(8,128)}) custom-call(bf16[128,1024]{1,0:T(8,128)(2,1)} %copy-done.2, f32[128,1024]{1,0:T(8,128)} %get-tuple-element.41.dy_ref, f32[128,128]{1,0:T(8,128)} %get-tuple-element.89.proj_ref, f32[8,2,128,128]{3,2,1,0:T(8,128)} %get-tuple-element.35.step_ref, ...), custom_call_target="tpu_custom_call" | custom-call | tf_op jit(solution)/shard_map/pallas_call | solution.py:435
  294.7 17.1 %shard_map.148 = (f32[128,1024]{1,0:T(8,128)}, f32[128,128]{1,0:T(8,128)}) custom-call(bf16[128,1024]{1,0:T(8,128)(2,1)} %copy-done.2, f32[128,1024]{1,0:T(8,128)} %get-tuple-element.41.dy_ref, f32[128,128]{1,0:T(8,128)} %get-tuple-element.90.proj_ref, f32[8,2,128,128]{3,2,1,0:T(8,128)} %get-tuple-element.32.step_ref, ...), custom_call_target="tpu_custom_call" | custom-call | tf_op jit(solution)/shard_map/pallas_call | solution.py:435
  316.7 5.3 %collective-permute-start.6 = (bf16[1,16,1024]{2,1,0:T(8,128)(2,1)S(1)}, bf16[1,16,1024]{2,1,0:T(8,128)(2,1)S(1)}, u32[]{:S(2)}, u32[]{:S(2)}) collective-permute-start(bf16[1,16,1024]{2,1,0:T(8,128)(2,1)S(1)} %get-tuple-element.78), channel_id=1, source_target_pairs={{8,0},{16,8},{24,16},{32,24},{40,32},{48,40},{56,48},{64,56},{72,6... | collective-permute-start | bytes 98312 | tf_op jit(solution)/shard_map/ppermute | solution.py:614
  323.7 3.7 collective-permute-start.7
  329.2 4.4 %collective-permute-done.8 = bf16[10,1,1024]{2,1,0:T(2,128)(2,1)S(1)} collective-permute-done((bf16[10,1,1024]{2,1,0:T(2,128)(2,1)S(1)}, bf16[10,1,1024]{2,1,0:T(2,128)(2,1)S(1)}, u32[]{:S(2)}, u32[]{:S(2)}) %collective-permute-start.8) | collective-permute-done | bytes 20512 | tf_op jit(solution)/shard_map/ppermute | solution.py:613
  335.9 7.0 %all-to-all-start.10 = ((bf16[128,8,512]{2,1,0:T(8,128)(2,1)}), bf16[128,8,512]{2,1,0:T(8,128)(2,1)}, u32[]{:S(2)}, u32[]{:S(2)}) async-start(bf16[128,8,512]{2,1,0:T(8,128)(2,1)} %bitcast.120), calls=%async_computation.10 | async-start | bytes 2097152 | tf_op jit(solution)/shard_map/all_to_all | solution.py:602
  345.4 21.5 %all-to-all-done.10 = bf16[128,8,512]{2,1,0:T(8,128)(2,1)} async-done(((bf16[128,8,512]{2,1,0:T(8,128)(2,1)}), bf16[128,8,512]{2,1,0:T(8,128)(2,1)}, u32[]{:S(2)}, u32[]{:S(2)}) %all-to-all-start.10) | async-done | bytes 1048608 | tf_op jit(solution)/shard_map/all_to_all | solution.py:602
  379.5 5.3 %all-to-all-done.11 = bf16[8,2,8,512]{3,2,1,0:T(8,128)(2,1)S(1)} async-done(((bf16[8,2,8,512]{3,2,1,0:T(8,128)(2,1)}), bf16[8,2,8,512]{3,2,1,0:T(8,128)(2,1)S(1)}, u32[]{:S(2)}, u32[]{:S(2)}) %all-to-all-start.11) | async-done | bytes 131104 | tf_op jit(solution)/shard_map/all_to_all | solution.py:579
  (171 shorter events, 85.4 us)
Async XLA Ops:
  7.2 48.7 %copy-start = (bf16[1024,256]{1,0:T(8,128)(2,1)S(1)}, bf16[1024,256]{1,0:T(8,128)(2,1)}, u32[]{:S(2)}) copy-start(bf16[1024,256]{1,0:T(8,128)(2,1)} %param.14) | copy-start | bytes 1572868
  7.2 117.6 %all-gather.9.cloned.1.call-start = ((), (), s32[]{:S(2)}) async-start(), calls=%async_computation.13 | async-start | bytes 1179648 | tf_op jit(solution)/shard_map/all_gather | solution.py:635
  8.7 20.8 %collective-permute-start.1 = (bf16[1,16,512]{2,1,0:T(8,128)(2,1)S(1)}, bf16[1,16,512]{2,1,0:T(8,128)(2,1)S(1)}, u32[]{:S(2)}, u32[]{:S(2)}) collective-permute-start(bf16[1,16,512]{2,1,0:T(8,128)(2,1)S(1)} %get-tuple-element.91), channel_id=1, source_target_pairs={{8,0},{16,8},{24,16},{32,24},{40,32},{48,40},{56,48},{64,56},{72,6... | collective-permute-start | bytes 49160 | tf_op jit(solution)/shard_map/ppermute | solution.py:614
  13.7 15.7 %collective-permute-start = (bf16[1,16,512]{2,1,0:T(8,128)(2,1)S(1)}, bf16[1,16,512]{2,1,0:T(8,128)(2,1)S(1)}, u32[]{:S(2)}, u32[]{:S(2)}) collective-permute-start(bf16[1,16,512]{2,1,0:T(8,128)(2,1)S(1)} %get-tuple-element.92), channel_id=1, source_target_pairs={{0,8},{8,16},{16,24},{24,32},{32,40},{40,48},{48,56},{56,64},{64,7... | collective-permute-start | bytes 49160 | tf_op jit(solution)/shard_map/ppermute | solution.py:613
  14.6 6.0 %collective-permute-start.4 = (bf16[256,128]{1,0:T(8,128)(2,1)S(1)}, bf16[256,128]{1,0:T(8,128)(2,1)S(1)}, u32[]{:S(2)}, u32[]{:S(2)}) collective-permute-start(bf16[256,128]{1,0:T(8,128)(2,1)S(1)} %broadcast_select_fusion.2), channel_id=1, source_target_pairs={{0,64},{8,72},{16,80},{24,88},{32,96},{40,104},{48,112},{56,120},{... | collective-permute-start | bytes 196616 | tf_op jit(solution)/shard_map/ppermute | solution.py:589
  18.8 35.4 %copy-start.26 = (f32[1,1,1024]{2,1,0:T(1,128)}, f32[1,1,1024]{2,1,0:T(1,128)S(1)}, u32[]{:S(2)}) copy-start(f32[1,1,1024]{2,1,0:T(1,128)S(1)} %get-tuple-element.97) | copy-start | bytes 12292
  18.9 35.4 %copy-start.28 = (f32[1,1,1024]{2,1,0:T(1,128)}, f32[1,1,1024]{2,1,0:T(1,128)S(1)}, u32[]{:S(2)}) copy-start(f32[1,1,1024]{2,1,0:T(1,128)S(1)} %get-tuple-element.98) | copy-start | bytes 12292
  18.9 35.4 %copy-start.30 = (f32[1,1,1024]{2,1,0:T(1,128)}, f32[1,1,1024]{2,1,0:T(1,128)S(1)}, u32[]{:S(2)}) copy-start(f32[1,1,1024]{2,1,0:T(1,128)S(1)} %get-tuple-element.99) | copy-start | bytes 12292
  18.9 35.4 %copy-start.32 = (f32[1,1,1024]{2,1,0:T(1,128)}, f32[1,1,1024]{2,1,0:T(1,128)S(1)}, u32[]{:S(2)}) copy-start(f32[1,1,1024]{2,1,0:T(1,128)S(1)} %get-tuple-element.100) | copy-start | bytes 12292
  18.9 35.4 %copy-start.34 = (f32[1,1,1024]{2,1,0:T(1,128)}, f32[1,1,1024]{2,1,0:T(1,128)S(1)}, u32[]{:S(2)}) copy-start(f32[1,1,1024]{2,1,0:T(1,128)S(1)} %get-tuple-element.101) | copy-start | bytes 12292
  23.2 29.3 %all-to-all-start = ((bf16[16,256,128]{2,1,0:T(8,128)(2,1)}), bf16[16,256,128]{2,1,0:T(8,128)(2,1)S(1)}, u32[]{:S(2)}, u32[]{:S(2)}) async-start(bf16[16,256,128]{2,1,0:T(8,128)(2,1)} %broadcast_in_dim.6), calls=%async_computation | async-start | bytes 2097152 | tf_op jit(solution)/shard_map/all_to_all | solution.py:579
  29.5 24.3 %collective-permute-start.2 = (bf16[10,1,512]{2,1,0:T(2,128)(2,1)S(1)}, bf16[10,1,512]{2,1,0:T(2,128)(2,1)S(1)}, u32[]{:S(2)}, u32[]{:S(2)}) collective-permute-start(bf16[10,1,512]{2,1,0:T(2,128)(2,1)S(1)} %get-tuple-element.87), channel_id=1, source_target_pairs={{0,1},{1,2},{2,3},{3,4},{4,5},{5,6},{6,7},{7,0},{8,9},{9,10},{10,1... | collective-permute-start | bytes 30728 | tf_op jit(solution)/shard_map/ppermute | solution.py:613
  31.5 22.3 %collective-permute-start.3 = (bf16[10,1,512]{2,1,0:T(2,128)(2,1)S(1)}, bf16[10,1,512]{2,1,0:T(2,128)(2,1)S(1)}, u32[]{:S(2)}, u32[]{:S(2)}) collective-permute-start(bf16[10,1,512]{2,1,0:T(2,128)(2,1)S(1)} %get-tuple-element.88), channel_id=1, source_target_pairs={{1,0},{2,1},{3,2},{4,3},{5,4},{6,5},{7,6},{0,7},{9,8},{10,9},{11,1... | collective-permute-start | bytes 30728 | tf_op jit(solution)/shard_map/ppermute | solution.py:614
  66.1 14.5 %all-to-all-start.3 = ((bf16[8,36,1024]{2,1,0:T(8,128)(2,1)}), bf16[8,36,1024]{2,1,0:T(8,128)(2,1)S(1)}, u32[]{:S(2)}, u32[]{:S(2)}) async-start(bf16[8,36,1024]{2,1,0:T(8,128)(2,1)} %get-tuple-element.36), calls=%async_computation.3 | async-start | bytes 1310720 | tf_op jit(solution)/shard_map/all_to_all | solution.py:579
  80.6 24.7 %all-to-all-start.1 = ((bf16[16,36,1024]{2,1,0:T(8,128)(2,1)}), bf16[16,36,1024]{2,1,0:T(8,128)(2,1)S(1)}, u32[]{:S(2)}, u32[]{:S(2)}) async-start(bf16[16,36,1024]{2,1,0:T(8,128)(2,1)} %get-tuple-element.33), calls=%async_computation.1 | async-start | bytes 2621440 | tf_op jit(solution)/shard_map/all_to_all | solution.py:579
  84.4 54.9 %all-gather.7.cloned.1.call-start = ((), (), s32[]{:S(2)}) async-start(), calls=%async_computation.12 | async-start | bytes 1114112 | tf_op jit(solution)/shard_map/all_gather | solution.py:642
  105.3 14.2 %all-to-all-start.4 = ((bf16[8,32,1024]{2,1,0:T(8,128)(2,1)}), bf16[8,32,1024]{2,1,0:T(8,128)(2,1)S(1)}, u32[]{:S(2)}, u32[]{:S(2)}) async-start(bf16[8,32,1024]{2,1,0:T(8,128)(2,1)} %shard_map.142), calls=%async_computation.4 | async-start | bytes 1048576 | tf_op jit(solution)/shard_map/all_to_all | solution.py:579
  120.4 22.8 %all-to-all-start.2 = ((bf16[16,32,1024]{2,1,0:T(8,128)(2,1)}), bf16[16,32,1024]{2,1,0:T(8,128)(2,1)S(1)}, u32[]{:S(2)}, u32[]{:S(2)}) async-start(bf16[16,32,1024]{2,1,0:T(8,128)(2,1)} %shard_map.139), calls=%async_computation.2 | async-start | bytes 2097152 | tf_op jit(solution)/shard_map/all_to_all | solution.py:579
  168.0 13.4 %all-to-all-start.7 = ((bf16[8,32,1024]{2,1,0:T(8,128)(2,1)}), bf16[8,32,1024]{2,1,0:T(8,128)(2,1)S(1)}, u32[]{:S(2)}, u32[]{:S(2)}) async-start(bf16[8,32,1024]{2,1,0:T(8,128)(2,1)} %shard_map.146), calls=%async_computation.7 | async-start | bytes 1048576 | tf_op jit(solution)/shard_map/all_to_all | solution.py:579
  181.4 25.0 %all-to-all-start.5 = ((bf16[16,32,1024]{2,1,0:T(8,128)(2,1)}), bf16[16,32,1024]{2,1,0:T(8,128)(2,1)S(1)}, u32[]{:S(2)}, u32[]{:S(2)}) async-start(bf16[16,32,1024]{2,1,0:T(8,128)(2,1)} %shard_map.144), calls=%async_computation.5 | async-start | bytes 2097152 | tf_op jit(solution)/shard_map/all_to_all | solution.py:579
  206.4 13.0 %all-to-all-start.8 = ((bf16[8,32,1024]{2,1,0:T(8,128)(2,1)}), bf16[8,32,1024]{2,1,0:T(8,128)(2,1)S(1)}, u32[]{:S(2)}, u32[]{:S(2)}) async-start(bf16[8,32,1024]{2,1,0:T(8,128)(2,1)} %shard_map.147), calls=%async_computation.8 | async-start | bytes 1048576 | tf_op jit(solution)/shard_map/all_to_all | solution.py:579
  219.4 21.6 %all-to-all-start.6 = ((bf16[16,32,1024]{2,1,0:T(8,128)(2,1)}), bf16[16,32,1024]{2,1,0:T(8,128)(2,1)S(1)}, u32[]{:S(2)}, u32[]{:S(2)}) async-start(bf16[16,32,1024]{2,1,0:T(8,128)(2,1)} %shard_map.145), calls=%async_computation.6 | async-start | bytes 2097152 | tf_op jit(solution)/shard_map/all_to_all | solution.py:579
  242.0 69.9 %all-to-all-start.9 = ((bf16[128,16,512]{2,1,0:T(8,128)(2,1)}), bf16[128,16,512]{2,1,0:T(8,128)(2,1)}, u32[]{:S(2)}, u32[]{:S(2)}) async-start(bf16[128,16,512]{2,1,0:T(8,128)(2,1)} %pad_maximum_fusion), calls=%async_computation.9 | async-start | bytes 4194304 | tf_op jit(solution)/shard_map/all_to_all | solution.py:602
  247.8 137.9 %all-gather.11.cloned.1.call-start = ((), (), s32[]{:S(2)}) async-start(), calls=%async_computation.14 | async-start | bytes 2228224 | tf_op jit(solution)/shard_map/all_gather | solution.py:730
  316.6 7.0 %collective-permute-start.5 = (bf16[1,16,1024]{2,1,0:T(8,128)(2,1)S(1)}, bf16[1,16,1024]{2,1,0:T(8,128)(2,1)S(1)}, u32[]{:S(2)}, u32[]{:S(2)}) collective-permute-start(bf16[1,16,1024]{2,1,0:T(8,128)(2,1)S(1)} %get-tuple-element.77), channel_id=1, source_target_pairs={{0,8},{8,16},{16,24},{24,32},{32,40},{40,48},{48,56},{56,64},{64,7... | collective-permute-start | bytes 98312 | tf_op jit(solution)/shard_map/ppermute | solution.py:613
  316.7 7.0 %collective-permute-start.6 = (bf16[1,16,1024]{2,1,0:T(8,128)(2,1)S(1)}, bf16[1,16,1024]{2,1,0:T(8,128)(2,1)S(1)}, u32[]{:S(2)}, u32[]{:S(2)}) collective-permute-start(bf16[1,16,1024]{2,1,0:T(8,128)(2,1)S(1)} %get-tuple-element.78), channel_id=1, source_target_pairs={{8,0},{16,8},{24,16},{32,24},{40,32},{48,40},{56,48},{64,56},{72,6... | collective-permute-start | bytes 98312 | tf_op jit(solution)/shard_map/ppermute | solution.py:614
  323.7 5.4 %collective-permute-start.7 = (bf16[10,1,1024]{2,1,0:T(2,128)(2,1)S(1)}, bf16[10,1,1024]{2,1,0:T(2,128)(2,1)S(1)}, u32[]{:S(2)}, u32[]{:S(2)}) collective-permute-start(bf16[10,1,1024]{2,1,0:T(2,128)(2,1)S(1)} %get-tuple-element.72), channel_id=1, source_target_pairs={{1,0},{2,1},{3,2},{4,3},{5,4},{6,5},{7,6},{0,7},{9,8},{10,9},{11,1... | collective-permute-start | bytes 61448 | tf_op jit(solution)/shard_map/ppermute | solution.py:614
  327.5 6.1 %collective-permute-start.8 = (bf16[10,1,1024]{2,1,0:T(2,128)(2,1)S(1)}, bf16[10,1,1024]{2,1,0:T(2,128)(2,1)S(1)}, u32[]{:S(2)}, u32[]{:S(2)}) collective-permute-start(bf16[10,1,1024]{2,1,0:T(2,128)(2,1)S(1)} %get-tuple-element.73), channel_id=1, source_target_pairs={{0,1},{1,2},{2,3},{3,4},{4,5},{5,6},{6,7},{7,0},{8,9},{9,10},{10,1... | collective-permute-start | bytes 61448 | tf_op jit(solution)/shard_map/ppermute | solution.py:613
  335.9 33.7 %copy-start.7 = (bf16[1024,512]{1,0:T(8,128)(2,1)S(1)}, bf16[1024,512]{1,0:T(8,128)(2,1)}, u32[]{:S(2)}) copy-start(bf16[1024,512]{1,0:T(8,128)(2,1)} %all-gather.9.cloned.1.call-done) | copy-start | bytes 3145732
  335.9 31.0 %all-to-all-start.10 = ((bf16[128,8,512]{2,1,0:T(8,128)(2,1)}), bf16[128,8,512]{2,1,0:T(8,128)(2,1)}, u32[]{:S(2)}, u32[]{:S(2)}) async-start(bf16[128,8,512]{2,1,0:T(8,128)(2,1)} %bitcast.120), calls=%async_computation.10 | async-start | bytes 2097152 | tf_op jit(solution)/shard_map/all_to_all | solution.py:602
  369.1 5.2 %collective-permute-start.9 = (bf16[8,512]{1,0:T(8,128)(2,1)S(1)}, bf16[8,512]{1,0:T(8,128)(2,1)S(1)}, u32[]{:S(2)}, u32[]{:S(2)}) collective-permute-start(bf16[8,512]{1,0:T(8,128)(2,1)S(1)} %get-tuple-element.102), channel_id=1, source_target_pairs={{0,64},{8,72},{16,80},{24,88},{32,96},{40,104},{48,112},{56,120},{... | collective-permute-start | bytes 24584 | tf_op jit(solution)/shard_map/ppermute | solution.py:589
  374.9 9.9 %all-to-all-start.11 = ((bf16[8,2,8,512]{3,2,1,0:T(8,128)(2,1)}), bf16[8,2,8,512]{3,2,1,0:T(8,128)(2,1)S(1)}, u32[]{:S(2)}, u32[]{:S(2)}) async-start(bf16[8,2,8,512]{3,2,1,0:T(8,128)(2,1)} %broadcast_in_dim.8), calls=%async_computation.11 | async-start | bytes 262144 | tf_op jit(solution)/shard_map/all_to_all | solution.py:579
  (31 other events, 241.2 us)
Sparse Core Ops, SparseCore 0:
  9.6 42.6 all-gather.8
  88.3 47.7 all-gather.6
  314.7 52.7 all-gather.10

commit v2 on v1

--- a/solution.py
+++ b/solution.py
@@ -589,9 +589,17 @@
     return lax.ppermute(shard, "row", [(i, (i + rows // 2) % rows) for i in range(rows)])
 
 
-def from_halves(pieces):
-    pieces = pieces.reshape(2, 8, C // 2, LANES)
-    return pieces.transpose(0, 2, 1, 3).reshape(C, E)
+def doubled(shard, axis):
+    gathered = shard[None]
+    for bit in range(lax.axis_size(axis).bit_length() - 1):
+        step = 1 << bit
+        swaps = [(i, i ^ step) for i in range(lax.axis_size(axis))]
+        other = lax.ppermute(gathered, axis, swaps)
+        later = (lax.axis_index(axis) & step) != 0
+        gathered = jnp.concatenate(
+            [jnp.where(later, other, gathered), jnp.where(later, gathered, other)]
+        )
+    return gathered
 
 
 def owner_order(part):
@@ -632,17 +640,15 @@
     grad_out,
 ):
     upper = lax.axis_index("row") >= lax.axis_size("row") // 2
-    out_full = lax.all_gather(out_weight, "col").reshape(E, C)
-    first, last = in_weight[: C // 2], in_weight[C // 2 :]
-    other = across(jnp.where(upper, first, last))
-    in_source = sent_to_all(jnp.where(upper, other, first), "row")
-    in_gate = jnp.where(upper, last, other)
-    in_source, in_gate = lax.optimization_barrier((in_source, in_gate))
-    in_source = from_halves(in_source)
-    in_gate = from_halves(lax.all_gather(in_gate, "row"))
+    field_tall = with_halo(field, (("row", 0),), 1)
+    in_pieces = sent_to_all(in_weight, "row")
+    in_pieces, out_weight = lax.optimization_barrier((in_pieces, out_weight))
+    in_source = in_pieces[:8].transpose(1, 0, 2).reshape(C, E)
+    in_gate = in_pieces[8:].transpose(1, 0, 2).reshape(C, E)
+    out_full = sent_to_all(out_weight, "col").reshape(E, C)
     field_rows = field.reshape(CELLS, C)
     grad_rows = grad_out.reshape(CELLS, C)
-    field_wide = with_halo(field, (("row", 0), ("col", 1)), 1)
+    field_wide = with_halo(field_tall, (("col", 1),), 1)
     padded = lax.dot_general(
         field_wide, in_source, (((2,), (0,)), ((), ())), preferred_element_type=F32
     ).astype(BF16)
@@ -656,9 +662,6 @@
     convolved = convolved.reshape(CELLS, E)
     active = jax.nn.silu(convolved).astype(BF16)
     projected = jnp.dot(active, proj_weight, preferred_element_type=F32)
-    back_mixed = lax.dot_general(
-        grad_rows, out_full, (((1,), (1,)), ((), ())), preferred_element_type=F32
-    )
 
     kinds = ((True, "row", 0), (False, "col", 2))
     width = R + 2 * N
@@ -679,6 +682,11 @@
         block_sums(down, active, projs[i], pads[i], dt_bias[k : k + 2], rates[i])
         for i, (down, _, k) in enumerate(kinds)
     ]
+    ends, out_full = lax.optimization_barrier((sums[1][0], out_full))
+    sums[1] = (ends, *sums[1][1:])
+    back_mixed = lax.dot_general(
+        grad_rows, out_full, (((1,), (1,)), ((), ())), preferred_element_type=F32
+    )
     infos = [swap(sums[i][0], axis) for i, (_, axis, _) in enumerate(kinds)]
     starts = [
         swap(closed(axis, infos[i], infos[i], rates[i], False), axis)
@@ -727,8 +735,7 @@
         for i, (down, _, _) in enumerate(kinds)
     ]
     done_piece, grads = lax.optimization_barrier((done_piece, grads))
-    grad_out_weight = lax.all_gather(jnp.pad(done_piece[:8], ((0, 56), (0, 0))), "row")
-    grad_out_weight = grad_out_weight[:, :8].reshape(E // 8, C)
+    grad_out_weight = doubled(done_piece[:8], "row").reshape(E // 8, C)
     gate_piece = done_piece[8:]
     proj_grads = jnp.concatenate([grads[i][1] + out_grads[i] for i in range(2)], axis=1)
     high, low = split(proj_grads)

time: 398 us -> 381 us (0.957)
  between operations: 14.5 us -> 1.63 us
  starting transfers between devices: 76 us -> 87.8 us
  waiting for transfers between devices: 122 us -> 112 us
    ppermute x4, waiting for transfers between devices: 5.99 us -> 26.3 us  [with_halo(): lax.ppermute(tail_part, axis, [(i, (i + 1) % count) for i in range(count)])]
    all_to_all x2, waiting for transfers between devices: 21.5 us -> 3.07 us  [reduced(): lax.all_to_all(pieces.reshape(128, rows, C), ('row', 'col'), 0, 0, tiled=...]
    all_to_all x10 -> x11, waiting for transfers between devices: 86.2 us -> 69.3 us  [swap(): return lax.all_to_all(x, axis, 0, 0, tiled=True)]
    all_to_all x10 -> x11, starting transfers between devices: 43.2 us -> 51.8 us  [swap(): return lax.all_to_all(x, axis, 0, 0, tiled=True)]
    ppermute x0 -> x4, waiting for transfers between devices: none -> 7.97 us  [doubled(): other = lax.ppermute(gathered, axis, swaps)]
    ppermute x0 -> x4, starting transfers between devices: none -> 4.31 us  [doubled(): other = lax.ppermute(gathered, axis, swaps)]
  transfers between devices with their start and end apart: 25 -> 26, of which waited for: 15 -> 15; matrix products, arithmetic and copies ran while one was open for 9% -> 9% of each run, Pallas kernels for 29% -> 30%
where the time goes in v2:
time: 381 us; the launch traced here: 377 us
  Pallas kernels  136 us (36%)
  waiting for transfers between devices  112 us (29%)
  starting transfers between devices  87.8 us (23%)
  local copies, waits for them, and re-layouts  16.6 us (4%)
  other arithmetic  12.2 us (3%)
  matrix products  11 us (3%)
    pallas_call x8, Pallas kernels, call(): pl.pallas_call(kernel, grid=(TILES,), in_specs=specs, out_specs=[spec for...  93.5 us
    all_to_all x11, waiting for transfers between devices, swap(): return lax.all_to_all(x, axis, 0, 0, tiled=True)  69.3 us
    all_to_all x11, starting transfers between devices, swap(): return lax.all_to_all(x, axis, 0, 0, tiled=True)  51.8 us
    pallas_call x2, Pallas kernels, block_out_grads(): pl.pallas_call(partial(out_grads_kernel, down=down), grid=(N,), in_specs=...  27.7 us
    ppermute x4, waiting for transfers between devices, with_halo(): lax.ppermute(tail_part, axis, [(i, (i + 1) % count) for i in range(count)])  26.3 us
    ppermute x4, starting transfers between devices, with_halo(): lax.ppermute(head, axis, [((i + 1) % count, i) for i in range(count)])  16.2 us
    all_to_all x2, starting transfers between devices, reduced(): lax.all_to_all(pieces.reshape(128, rows, C), ('row', 'col'), 0, 0, tiled=...  12.4 us
    pallas_call x4, Pallas kernels, closed(): pl.pallas_call(partial(close_kernel, peers=peers, flip=flip), grid=(E //...  11.1 us
  transfers between devices with their start and end apart: 26, of which 15 were waited for; matrix products, arithmetic and copies ran while one was open for 9% of the time, Pallas kernels for 30%

profile of v2, /device:TPU:0, one launch (start us, length us, event | category | flops | bytes accessed | tf_op | source)
XLA Modules:
  0.0 377.4 jit_solution(8021815216137501177)
XLA Ops:
  3.3 7.3 %all-to-all-start = ((bf16[16,512,128]{2,1,0:T(8,128)(2,1)}), bf16[16,512,128]{2,1,0:T(8,128)(2,1)S(1)}, u32[]{:S(2)}, u32[]{:S(2)}) async-start(bf16[16,512,128]{2,1,0:T(8,128)(2,1)} %broadcast_in_dim.10), calls=%async_computation | async-start | bytes 4194304 | tf_op jit(solution)/shard_map/all_to_all | solution.py:579
  10.7 5.3 %collective-permute-start.1 = (bf16[1,16,512]{2,1,0:T(8,128)(2,1)S(1)}, bf16[1,16,512]{2,1,0:T(8,128)(2,1)S(1)}, u32[]{:S(2)}, u32[]{:S(2)}) collective-permute-start(bf16[1,16,512]{2,1,0:T(8,128)(2,1)S(1)} %get-tuple-element.99), channel_id=1, source_target_pairs={{8,0},{16,8},{24,16},{32,24},{40,32},{48,40},{56,48},{64,56},{72,6... | collective-permute-start | bytes 49160 | tf_op jit(solution)/shard_map/ppermute | solution.py:622
  19.3 20.4 %collective-permute-done = bf16[1,16,512]{2,1,0:T(8,128)(2,1)S(1)} collective-permute-done((bf16[1,16,512]{2,1,0:T(8,128)(2,1)S(1)}, bf16[1,16,512]{2,1,0:T(8,128)(2,1)S(1)}, u32[]{:S(2)}, u32[]{:S(2)}) %collective-permute-start) | collective-permute-done | bytes 16416 | tf_op jit(solution)/shard_map/ppermute | solution.py:621
  45.2 4.2 %all-to-all-start.3 = ((bf16[8,128,512]{2,1,0:T(8,128)(2,1)}), bf16[8,128,512]{2,1,0:T(8,128)(2,1)}, u32[]{:S(2)}, u32[]{:S(2)}) async-start(bf16[8,128,512]{2,1,0:T(8,128)(2,1)} %broadcast_in_dim.11), calls=%async_computation.3 | async-start | bytes 2097152 | tf_op jit(solution)/shard_map/all_to_all | solution.py:579
  55.0 9.4 %shard_map.141 = (bf16[8,36,1024]{2,1,0:T(8,128)(2,1)}, f32[8,2,128,128]{3,2,1,0:T(8,128)}, f32[8,2,128,128]{3,2,1,0:T(8,128)}) custom-call(bf16[128,1024]{1,0:T(8,128)(2,1)} %copy-done.2, f32[128,128]{1,0:T(8,128)} %get-tuple-element.97.proj_ref, bf16[2,128,1024]{2,1,0:T(8,128)(2,1)} %pad_maximum_fusion.5.dtw_ref, f32[2,1024]{1,0:T(2,128)} %get-tuple-element.118.bias_ref, ...), custom_call_target="tpu_custom_call" | custom-call | tf_op jit(solution)/shard_map/pallas_call | solution.py:435
  64.4 5.6 %all-to-all-start.4 = ((bf16[8,36,1024]{2,1,0:T(8,128)(2,1)}), bf16[8,36,1024]{2,1,0:T(8,128)(2,1)S(1)}, u32[]{:S(2)}, u32[]{:S(2)}) async-start(bf16[8,36,1024]{2,1,0:T(8,128)(2,1)} %get-tuple-element.40), calls=%async_computation.4 | async-start | bytes 1310720 | tf_op jit(solution)/shard_map/all_to_all | solution.py:579
  70.9 8.8 %shard_map.138 = (bf16[16,36,1024]{2,1,0:T(8,128)(2,1)}, f32[8,2,128,128]{3,2,1,0:T(8,128)}, f32[8,2,128,128]{3,2,1,0:T(8,128)}) custom-call(bf16[128,1024]{1,0:T(8,128)(2,1)} %copy-done.2, f32[128,128]{1,0:T(8,128)} %get-tuple-element.98.proj_ref, bf16[2,128,1024]{2,1,0:T(8,128)(2,1)} %pad_maximum_fusion.4.dtw_ref, f32[2,1024]{1,0:T(2,128)} %get-tuple-element.119.bias_ref, ...), custom_call_target="tpu_custom_call" | custom-call | tf_op jit(solution)/shard_map/pallas_call | solution.py:435
  80.1 3.9 %all-to-all-start.1 = ((bf16[16,36,1024]{2,1,0:T(8,128)(2,1)}), bf16[16,36,1024]{2,1,0:T(8,128)(2,1)S(1)}, u32[]{:S(2)}, u32[]{:S(2)}) async-start(bf16[16,36,1024]{2,1,0:T(8,128)(2,1)} %get-tuple-element.35), calls=%async_computation.1 | async-start | bytes 2621440 | tf_op jit(solution)/shard_map/all_to_all | solution.py:579
  86.3 18.5 %all-to-all-done.1.info_ref.ends_ref = bf16[16,36,1024]{2,1,0:T(8,128)(2,1)S(1)} async-done(((bf16[16,36,1024]{2,1,0:T(8,128)(2,1)}), bf16[16,36,1024]{2,1,0:T(8,128)(2,1)S(1)}, u32[]{:S(2)}, u32[]{:S(2)}) %all-to-all-start.1) | async-done | bytes 1179680 | tf_op jit(solution)/shard_map/all_to_all | solution.py:579
  104.8 5.2 %all-to-all-start.5 = ((bf16[8,32,1024]{2,1,0:T(8,128)(2,1)}), bf16[8,32,1024]{2,1,0:T(8,128)(2,1)S(1)}, u32[]{:S(2)}, u32[]{:S(2)}) async-start(bf16[8,32,1024]{2,1,0:T(8,128)(2,1)} %shard_map.142), calls=%async_computation.5 | async-start | bytes 1048576 | tf_op jit(solution)/shard_map/all_to_all | solution.py:579
  113.2 6.1 %all-to-all-done.5.start_ref = bf16[8,32,1024]{2,1,0:T(8,128)(2,1)S(1)} async-done(((bf16[8,32,1024]{2,1,0:T(8,128)(2,1)}), bf16[8,32,1024]{2,1,0:T(8,128)(2,1)S(1)}, u32[]{:S(2)}, u32[]{:S(2)}) %all-to-all-start.5) | async-done | bytes 524320 | tf_op jit(solution)/shard_map/all_to_all | solution.py:579
  119.3 4.5 %all-to-all-start.2 = ((bf16[16,32,1024]{2,1,0:T(8,128)(2,1)}), bf16[16,32,1024]{2,1,0:T(8,128)(2,1)}, u32[]{:S(2)}, u32[]{:S(2)}) async-start(bf16[16,32,1024]{2,1,0:T(8,128)(2,1)} %shard_map.139), calls=%async_computation.2 | async-start | bytes 2097152 | tf_op jit(solution)/shard_map/all_to_all | solution.py:579
  132.1 11.9 %shard_map.143 = (f32[128,1024]{1,0:T(8,128)}, f32[8,2,16,136,128]{4,3,2,1,0:T(8,128)}) custom-call(bf16[128,1024]{1,0:T(8,128)(2,1)} %copy-done.2, f32[128,128]{1,0:T(8,128)} %get-tuple-element.97.proj_ref, f32[8,2,128,128]{3,2,1,0:T(8,128)} %get-tuple-element.37.step_ref, f32[2,16,1024]{2,1,0:T(8,128)} %get-tuple-element.87.rate_ref, ...), custom_call_target="tpu_custom_call" | custom-call | tf_op jit(solution)/shard_map/pallas_call | solution.py:435
  144.1 12.1 %shard_map.140 = (f32[128,1024]{1,0:T(8,128)}, f32[8,2,16,144,128]{4,3,2,1,0:T(8,128)}) custom-call(bf16[128,1024]{1,0:T(8,128)(2,1)} %copy-done.2, f32[128,128]{1,0:T(8,128)} %get-tuple-element.98.proj_ref, f32[8,2,128,128]{3,2,1,0:T(8,128)} %get-tuple-element.34.step_ref, f32[2,16,1024]{2,1,0:T(8,128)} %get-tuple-element.88.rate_ref, ...), custom_call_target="tpu_custom_call" | custom-call | tf_op jit(solution)/shard_map/pallas_call | solution.py:435
  156.2 4.1 %tail.1 = (bf16[128,1024]{1,0:T(8,128)(2,1)}, f32[128,1024]{1,0:T(8,128)}, bf16[128,1024]{1,0:T(8,128)(2,1)}) custom-call(f32[128,1024]{1,0:T(8,128)} %get-tuple-element.36.y0_ref, f32[128,1024]{1,0:T(8,128)} %get-tuple-element.41.y1_ref, bf16[128,1024]{1,0:T(8,128)(2,1)} %fusion.1.gate_ref, f32[1,1024]{1,0:T(1,128)} %bitcast.156, ...), custom_call_target="tpu_custom_call" | custom-call | tf_op jit(solution)/shard_map/tail/pallas_call | solution.py:563
  160.3 7.7 %shard_map.146 = bf16[8,32,1024]{2,1,0:T(8,128)(2,1)} custom-call(f32[128,1024]{1,0:T(8,128)} %get-tuple-element.45.dy_ref, f32[128,128]{1,0:T(8,128)} %get-tuple-element.97.proj_ref, f32[8,2,128,128]{3,2,1,0:T(8,128)} %get-tuple-element.37.step_ref, f32[2,16,1024]{2,1,0:T(8,128)} %get-tuple-element.87.rate_ref), custom_call_target="tpu_custom_call" | custom-call | tf_op jit(solution)/shard_map/pallas_call | solution.py:435
  171.4 7.5 %shard_map.144 = bf16[16,32,1024]{2,1,0:T(8,128)(2,1)} custom-call(f32[128,1024]{1,0:T(8,128)} %get-tuple-element.45.dy_ref, f32[128,128]{1,0:T(8,128)} %get-tuple-element.98.proj_ref, f32[8,2,128,128]{3,2,1,0:T(8,128)} %get-tuple-element.34.step_ref, f32[2,16,1024]{2,1,0:T(8,128)} %get-tuple-element.88.rate_ref), custom_call_target="tpu_custom_call" | custom-call | tf_op jit(solution)/shard_map/pallas_call | solution.py:435
  181.3 7.0 %all-to-all-start.6 = ((bf16[16,32,1024]{2,1,0:T(8,128)(2,1)}), bf16[16,32,1024]{2,1,0:T(8,128)(2,1)S(1)}, u32[]{:S(2)}, u32[]{:S(2)}) async-start(bf16[16,32,1024]{2,1,0:T(8,128)(2,1)} %shard_map.144), calls=%async_computation.6 | async-start | bytes 2097152 | tf_op jit(solution)/shard_map/all_to_all | solution.py:579
  190.6 15.7 %all-to-all-done.6.ends_ref = bf16[16,32,1024]{2,1,0:T(8,128)(2,1)S(1)} async-done(((bf16[16,32,1024]{2,1,0:T(8,128)(2,1)}), bf16[16,32,1024]{2,1,0:T(8,128)(2,1)S(1)}, u32[]{:S(2)}, u32[]{:S(2)}) %all-to-all-start.6) | async-done | bytes 1048608 | tf_op jit(solution)/shard_map/all_to_all | solution.py:579
  213.0 6.3 %all-to-all-done.9.tail_ref = bf16[8,32,1024]{2,1,0:T(8,128)(2,1)S(1)} async-done(((bf16[8,32,1024]{2,1,0:T(8,128)(2,1)}), bf16[8,32,1024]{2,1,0:T(8,128)(2,1)S(1)}, u32[]{:S(2)}, u32[]{:S(2)}) %all-to-all-start.9) | async-done | bytes 524320 | tf_op jit(solution)/shard_map/all_to_all | solution.py:579
  226.7 14.2 %all-to-all-done.7.tail_ref = bf16[16,32,1024]{2,1,0:T(8,128)(2,1)S(1)} async-done(((bf16[16,32,1024]{2,1,0:T(8,128)(2,1)}), bf16[16,32,1024]{2,1,0:T(8,128)(2,1)S(1)}, u32[]{:S(2)}, u32[]{:S(2)}) %all-to-all-start.7) | async-done | bytes 1048608 | tf_op jit(solution)/shard_map/all_to_all | solution.py:579
  241.9 6.0 %all-to-all-start.10 = ((bf16[128,16,512]{2,1,0:T(8,128)(2,1)}), bf16[128,16,512]{2,1,0:T(8,128)(2,1)}, u32[]{:S(2)}, u32[]{:S(2)}) async-start(bf16[128,16,512]{2,1,0:T(8,128)(2,1)} %pad_maximum_fusion), calls=%async_computation.10 | async-start | bytes 4194304 | tf_op jit(solution)/shard_map/all_to_all | solution.py:610
  247.9 13.8 %out_grads_across.1 = f32[128,128]{1,0:T(8,128)} custom-call(f32[128,1024]{1,0:T(8,128)} %get-tuple-element.45.dy_ref, f32[8,2,16,136,128]{4,3,2,1,0:T(8,128)} %get-tuple-element.53.hs_ref), custom_call_target="tpu_custom_call" | custom-call | tf_op jit(solution)/shard_map/out_grads_across/pallas_call | solution.py:527
  261.7 13.9 %out_grads_down.1 = f32[128,128]{1,0:T(8,128)} custom-call(f32[128,1024]{1,0:T(8,128)} %get-tuple-element.45.dy_ref, f32[8,2,16,144,128]{4,3,2,1,0:T(8,128)} %get-tuple-element.48.hs_ref), custom_call_target="tpu_custom_call" | custom-call | tf_op jit(solution)/shard_map/out_grads_down/pallas_call | solution.py:527
  275.9 19.0 %shard_map.149 = (f32[128,1024]{1,0:T(8,128)}, f32[128,128]{1,0:T(8,128)}) custom-call(bf16[128,1024]{1,0:T(8,128)(2,1)} %copy-done.2, f32[128,1024]{1,0:T(8,128)} %get-tuple-element.45.dy_ref, f32[128,128]{1,0:T(8,128)} %get-tuple-element.97.proj_ref, f32[8,2,128,128]{3,2,1,0:T(8,128)} %get-tuple-element.37.step_ref, ...), custom_call_target="tpu_custom_call" | custom-call | tf_op jit(solution)/shard_map/pallas_call | solution.py:435
  294.9 17.1 %shard_map.148 = (f32[128,1024]{1,0:T(8,128)}, f32[128,128]{1,0:T(8,128)}) custom-call(bf16[128,1024]{1,0:T(8,128)(2,1)} %copy-done.2, f32[128,1024]{1,0:T(8,128)} %get-tuple-element.45.dy_ref, f32[128,128]{1,0:T(8,128)} %get-tuple-element.98.proj_ref, f32[8,2,128,128]{3,2,1,0:T(8,128)} %get-tuple-element.34.step_ref, ...), custom_call_target="tpu_custom_call" | custom-call | tf_op jit(solution)/shard_map/pallas_call | solution.py:435
  315.7 4.9 %collective-permute-start.5 = (bf16[1,16,1024]{2,1,0:T(8,128)(2,1)S(1)}, bf16[1,16,1024]{2,1,0:T(8,128)(2,1)S(1)}, u32[]{:S(2)}, u32[]{:S(2)}) collective-permute-start(bf16[1,16,1024]{2,1,0:T(8,128)(2,1)S(1)} %get-tuple-element.86), channel_id=1, source_target_pairs={{8,0},{16,8},{24,16},{32,24},{40,32},{48,40},{56,48},{64,56},{72,6... | collective-permute-start | bytes 98312 | tf_op jit(solution)/shard_map/ppermute | solution.py:622
  327.7 4.4 %collective-permute-done.7 = bf16[10,1,1024]{2,1,0:T(2,128)(2,1)S(1)} collective-permute-done((bf16[10,1,1024]{2,1,0:T(2,128)(2,1)S(1)}, bf16[10,1,1024]{2,1,0:T(2,128)(2,1)S(1)}, u32[]{:S(2)}, u32[]{:S(2)}) %collective-permute-start.7) | collective-permute-done | bytes 20512 | tf_op jit(solution)/shard_map/ppermute | solution.py:621
  334.4 6.4 %all-to-all-start.11 = ((bf16[128,8,512]{2,1,0:T(8,128)(2,1)}), bf16[128,8,512]{2,1,0:T(8,128)(2,1)S(1)}, u32[]{:S(2)}, u32[]{:S(2)}) async-start(bf16[128,8,512]{2,1,0:T(8,128)(2,1)} %bitcast.121), calls=%async_computation.11 | async-start | bytes 2097152 | tf_op jit(solution)/shard_map/all_to_all | solution.py:610
  346.0 8.0 %collective-permute-done.11 = f32[4,8,512]{2,1,0:T(8,128)S(1)} collective-permute-done((f32[4,8,512]{2,1,0:T(8,128)S(1)}, f32[4,8,512]{2,1,0:T(8,128)S(1)}, u32[]{:S(2)}, u32[]{:S(2)}) %collective-permute-start.11) | collective-permute-done | bytes 65568 | tf_op jit(solution)/shard_map/ppermute | solution.py:597
  361.1 4.7 %collective-permute-done.8 = bf16[8,512]{1,0:T(8,128)(2,1)S(1)} collective-permute-done((bf16[8,512]{1,0:T(8,128)(2,1)S(1)}, bf16[8,512]{1,0:T(8,128)(2,1)S(1)}, u32[]{:S(2)}, u32[]{:S(2)}) %collective-permute-start.8) | collective-permute-done | bytes 8224 | tf_op jit(solution)/shard_map/ppermute | solution.py:589
  370.6 5.9 %all-to-all-done.12 = bf16[8,2,8,512]{3,2,1,0:T(8,128)(2,1)S(1)} async-done(((bf16[8,2,8,512]{3,2,1,0:T(8,128)(2,1)}), bf16[8,2,8,512]{3,2,1,0:T(8,128)(2,1)S(1)}, u32[]{:S(2)}, u32[]{:S(2)}) %all-to-all-start.12) | async-done | bytes 131104 | tf_op jit(solution)/shard_map/all_to_all | solution.py:579
  (201 shorter events, 86.2 us)
Async XLA Ops:
  0.6 53.5 %copy-start = (bf16[1024,256]{1,0:T(8,128)(2,1)S(1)}, bf16[1024,256]{1,0:T(8,128)(2,1)}, u32[]{:S(2)}) copy-start(bf16[1024,256]{1,0:T(8,128)(2,1)} %param.14) | copy-start | bytes 1572868
  3.3 40.8 %all-to-all-start = ((bf16[16,512,128]{2,1,0:T(8,128)(2,1)}), bf16[16,512,128]{2,1,0:T(8,128)(2,1)S(1)}, u32[]{:S(2)}, u32[]{:S(2)}) async-start(bf16[16,512,128]{2,1,0:T(8,128)(2,1)} %broadcast_in_dim.10), calls=%async_computation | async-start | bytes 4194304 | tf_op jit(solution)/shard_map/all_to_all | solution.py:579
  10.7 29.0 %collective-permute-start.1 = (bf16[1,16,512]{2,1,0:T(8,128)(2,1)S(1)}, bf16[1,16,512]{2,1,0:T(8,128)(2,1)S(1)}, u32[]{:S(2)}, u32[]{:S(2)}) collective-permute-start(bf16[1,16,512]{2,1,0:T(8,128)(2,1)S(1)} %get-tuple-element.99), channel_id=1, source_target_pairs={{8,0},{16,8},{24,16},{32,24},{40,32},{48,40},{56,48},{64,56},{72,6... | collective-permute-start | bytes 49160 | tf_op jit(solution)/shard_map/ppermute | solution.py:622
  16.0 23.7 %collective-permute-start = (bf16[1,16,512]{2,1,0:T(8,128)(2,1)S(1)}, bf16[1,16,512]{2,1,0:T(8,128)(2,1)S(1)}, u32[]{:S(2)}, u32[]{:S(2)}) collective-permute-start(bf16[1,16,512]{2,1,0:T(8,128)(2,1)S(1)} %get-tuple-element.100), channel_id=1, source_target_pairs={{0,8},{8,16},{16,24},{24,32},{32,40},{40,48},{48,56},{56,64},{64,7... | collective-permute-start | bytes 49160 | tf_op jit(solution)/shard_map/ppermute | solution.py:621
  17.6 34.8 %copy-start.30 = (f32[1,1,1024]{2,1,0:T(1,128)}, f32[1,1,1024]{2,1,0:T(1,128)S(1)}, u32[]{:S(2)}) copy-start(f32[1,1,1024]{2,1,0:T(1,128)S(1)} %get-tuple-element.105) | copy-start | bytes 12292
  17.6 34.8 %copy-start.32 = (f32[1,1,1024]{2,1,0:T(1,128)}, f32[1,1,1024]{2,1,0:T(1,128)S(1)}, u32[]{:S(2)}) copy-start(f32[1,1,1024]{2,1,0:T(1,128)S(1)} %get-tuple-element.106) | copy-start | bytes 12292
  17.7 34.8 %copy-start.34 = (f32[1,1,1024]{2,1,0:T(1,128)}, f32[1,1,1024]{2,1,0:T(1,128)S(1)}, u32[]{:S(2)}) copy-start(f32[1,1,1024]{2,1,0:T(1,128)S(1)} %get-tuple-element.107) | copy-start | bytes 12292
  17.7 34.8 %copy-start.36 = (f32[1,1,1024]{2,1,0:T(1,128)}, f32[1,1,1024]{2,1,0:T(1,128)S(1)}, u32[]{:S(2)}) copy-start(f32[1,1,1024]{2,1,0:T(1,128)S(1)} %get-tuple-element.108) | copy-start | bytes 12292
  17.7 34.8 %copy-start.38 = (f32[1,1,1024]{2,1,0:T(1,128)}, f32[1,1,1024]{2,1,0:T(1,128)S(1)}, u32[]{:S(2)}) copy-start(f32[1,1,1024]{2,1,0:T(1,128)S(1)} %get-tuple-element.109) | copy-start | bytes 12292
  39.8 12.2 %collective-permute-start.2 = (bf16[10,1,512]{2,1,0:T(2,128)(2,1)S(1)}, bf16[10,1,512]{2,1,0:T(2,128)(2,1)S(1)}, u32[]{:S(2)}, u32[]{:S(2)}) collective-permute-start(bf16[10,1,512]{2,1,0:T(2,128)(2,1)S(1)} %get-tuple-element.93), channel_id=1, source_target_pairs={{0,1},{1,2},{2,3},{3,4},{4,5},{5,6},{6,7},{7,0},{8,9},{9,10},{10,1... | collective-permute-start | bytes 30728 | tf_op jit(solution)/shard_map/ppermute | solution.py:621
  41.8 10.2 %collective-permute-start.3 = (bf16[10,1,512]{2,1,0:T(2,128)(2,1)S(1)}, bf16[10,1,512]{2,1,0:T(2,128)(2,1)S(1)}, u32[]{:S(2)}, u32[]{:S(2)}) collective-permute-start(bf16[10,1,512]{2,1,0:T(2,128)(2,1)S(1)} %get-tuple-element.94), channel_id=1, source_target_pairs={{1,0},{2,1},{3,2},{4,3},{5,4},{6,5},{7,6},{0,7},{9,8},{10,9},{11,1... | collective-permute-start | bytes 30728 | tf_op jit(solution)/shard_map/ppermute | solution.py:622
  45.2 19.1 %all-to-all-start.3 = ((bf16[8,128,512]{2,1,0:T(8,128)(2,1)}), bf16[8,128,512]{2,1,0:T(8,128)(2,1)}, u32[]{:S(2)}, u32[]{:S(2)}) async-start(bf16[8,128,512]{2,1,0:T(8,128)(2,1)} %broadcast_in_dim.11), calls=%async_computation.3 | async-start | bytes 2097152 | tf_op jit(solution)/shard_map/all_to_all | solution.py:579
  64.4 15.7 %all-to-all-start.4 = ((bf16[8,36,1024]{2,1,0:T(8,128)(2,1)}), bf16[8,36,1024]{2,1,0:T(8,128)(2,1)S(1)}, u32[]{:S(2)}, u32[]{:S(2)}) async-start(bf16[8,36,1024]{2,1,0:T(8,128)(2,1)} %get-tuple-element.40), calls=%async_computation.4 | async-start | bytes 1310720 | tf_op jit(solution)/shard_map/all_to_all | solution.py:579
  80.1 24.7 %all-to-all-start.1 = ((bf16[16,36,1024]{2,1,0:T(8,128)(2,1)}), bf16[16,36,1024]{2,1,0:T(8,128)(2,1)S(1)}, u32[]{:S(2)}, u32[]{:S(2)}) async-start(bf16[16,36,1024]{2,1,0:T(8,128)(2,1)} %get-tuple-element.35), calls=%async_computation.1 | async-start | bytes 2621440 | tf_op jit(solution)/shard_map/all_to_all | solution.py:579
  104.8 14.5 %all-to-all-start.5 = ((bf16[8,32,1024]{2,1,0:T(8,128)(2,1)}), bf16[8,32,1024]{2,1,0:T(8,128)(2,1)S(1)}, u32[]{:S(2)}, u32[]{:S(2)}) async-start(bf16[8,32,1024]{2,1,0:T(8,128)(2,1)} %shard_map.142), calls=%async_computation.5 | async-start | bytes 1048576 | tf_op jit(solution)/shard_map/all_to_all | solution.py:579
  119.3 24.8 %all-to-all-start.2 = ((bf16[16,32,1024]{2,1,0:T(8,128)(2,1)}), bf16[16,32,1024]{2,1,0:T(8,128)(2,1)}, u32[]{:S(2)}, u32[]{:S(2)}) async-start(bf16[16,32,1024]{2,1,0:T(8,128)(2,1)} %shard_map.139), calls=%async_computation.2 | async-start | bytes 2097152 | tf_op jit(solution)/shard_map/all_to_all | solution.py:579
  167.9 13.3 %all-to-all-start.8 = ((bf16[8,32,1024]{2,1,0:T(8,128)(2,1)}), bf16[8,32,1024]{2,1,0:T(8,128)(2,1)S(1)}, u32[]{:S(2)}, u32[]{:S(2)}) async-start(bf16[8,32,1024]{2,1,0:T(8,128)(2,1)} %shard_map.146), calls=%async_computation.8 | async-start | bytes 1048576 | tf_op jit(solution)/shard_map/all_to_all | solution.py:579
  181.3 25.0 %all-to-all-start.6 = ((bf16[16,32,1024]{2,1,0:T(8,128)(2,1)}), bf16[16,32,1024]{2,1,0:T(8,128)(2,1)S(1)}, u32[]{:S(2)}, u32[]{:S(2)}) async-start(bf16[16,32,1024]{2,1,0:T(8,128)(2,1)} %shard_map.144), calls=%async_computation.6 | async-start | bytes 2097152 | tf_op jit(solution)/shard_map/all_to_all | solution.py:579
  206.3 13.0 %all-to-all-start.9 = ((bf16[8,32,1024]{2,1,0:T(8,128)(2,1)}), bf16[8,32,1024]{2,1,0:T(8,128)(2,1)S(1)}, u32[]{:S(2)}, u32[]{:S(2)}) async-start(bf16[8,32,1024]{2,1,0:T(8,128)(2,1)} %shard_map.147), calls=%async_computation.9 | async-start | bytes 1048576 | tf_op jit(solution)/shard_map/all_to_all | solution.py:579
  219.3 21.6 %all-to-all-start.7 = ((bf16[16,32,1024]{2,1,0:T(8,128)(2,1)}), bf16[16,32,1024]{2,1,0:T(8,128)(2,1)S(1)}, u32[]{:S(2)}, u32[]{:S(2)}) async-start(bf16[16,32,1024]{2,1,0:T(8,128)(2,1)} %shard_map.145), calls=%async_computation.7 | async-start | bytes 2097152 | tf_op jit(solution)/shard_map/all_to_all | solution.py:579
  241.9 70.2 %all-to-all-start.10 = ((bf16[128,16,512]{2,1,0:T(8,128)(2,1)}), bf16[128,16,512]{2,1,0:T(8,128)(2,1)}, u32[]{:S(2)}, u32[]{:S(2)}) async-start(bf16[128,16,512]{2,1,0:T(8,128)(2,1)} %pad_maximum_fusion), calls=%async_computation.10 | async-start | bytes 4194304 | tf_op jit(solution)/shard_map/all_to_all | solution.py:610
  314.3 6.4 %collective-permute-start.9 = (f32[1,8,512]{2,1,0:T(8,128)S(1)}, f32[1,8,512]{2,1,0:T(8,128)S(1)}, u32[]{:S(2)}, u32[]{:S(2)}) collective-permute-start(f32[1,8,512]{2,1,0:T(8,128)S(1)} %slice_bitcast_fusion.8), channel_id=1, source_target_pairs={{0,8},{8,0},{16,24},{24,16},{32,40},{40,32},{48,56},{56,48},{64,72... | collective-permute-start | bytes 49160 | tf_op jit(solution)/shard_map/ppermute | solution.py:597
  315.2 7.0 %collective-permute-start.4 = (bf16[1,16,1024]{2,1,0:T(8,128)(2,1)S(1)}, bf16[1,16,1024]{2,1,0:T(8,128)(2,1)S(1)}, u32[]{:S(2)}, u32[]{:S(2)}) collective-permute-start(bf16[1,16,1024]{2,1,0:T(8,128)(2,1)S(1)} %get-tuple-element.85), channel_id=1, source_target_pairs={{0,8},{8,16},{16,24},{24,32},{32,40},{40,48},{48,56},{56,64},{64,7... | collective-permute-start | bytes 98312 | tf_op jit(solution)/shard_map/ppermute | solution.py:621
  315.7 6.5 %collective-permute-start.5 = (bf16[1,16,1024]{2,1,0:T(8,128)(2,1)S(1)}, bf16[1,16,1024]{2,1,0:T(8,128)(2,1)S(1)}, u32[]{:S(2)}, u32[]{:S(2)}) collective-permute-start(bf16[1,16,1024]{2,1,0:T(8,128)(2,1)S(1)} %get-tuple-element.86), channel_id=1, source_target_pairs={{8,0},{16,8},{24,16},{32,24},{40,32},{48,40},{56,48},{64,56},{72,6... | collective-permute-start | bytes 98312 | tf_op jit(solution)/shard_map/ppermute | solution.py:622
  322.3 5.3 %collective-permute-start.6 = (bf16[10,1,1024]{2,1,0:T(2,128)(2,1)S(1)}, bf16[10,1,1024]{2,1,0:T(2,128)(2,1)S(1)}, u32[]{:S(2)}, u32[]{:S(2)}) collective-permute-start(bf16[10,1,1024]{2,1,0:T(2,128)(2,1)S(1)} %get-tuple-element.78), channel_id=1, source_target_pairs={{1,0},{2,1},{3,2},{4,3},{5,4},{6,5},{7,6},{0,7},{9,8},{10,9},{11,1... | collective-permute-start | bytes 61448 | tf_op jit(solution)/shard_map/ppermute | solution.py:622
  325.9 6.1 %collective-permute-start.7 = (bf16[10,1,1024]{2,1,0:T(2,128)(2,1)S(1)}, bf16[10,1,1024]{2,1,0:T(2,128)(2,1)S(1)}, u32[]{:S(2)}, u32[]{:S(2)}) collective-permute-start(bf16[10,1,1024]{2,1,0:T(2,128)(2,1)S(1)} %get-tuple-element.79), channel_id=1, source_target_pairs={{0,1},{1,2},{2,3},{3,4},{4,5},{5,6},{6,7},{7,0},{8,9},{9,10},{10,1... | collective-permute-start | bytes 61448 | tf_op jit(solution)/shard_map/ppermute | solution.py:621
  326.6 16.5 %collective-permute-start.10 = (f32[2,8,512]{2,1,0:T(8,128)}, f32[2,8,512]{2,1,0:T(8,128)}, u32[]{:S(2)}, u32[]{:S(2)}) collective-permute-start(f32[2,8,512]{2,1,0:T(8,128)} %pad_maximum_fusion.11), channel_id=1, source_target_pairs={{0,16},{8,24},{16,0},{24,8},{32,48},{40,56},{48,32},{56,40},{64,80... | collective-permute-start | bytes 98312 | tf_op jit(solution)/shard_map/ppermute | solution.py:597
  334.4 25.3 %all-to-all-start.11 = ((bf16[128,8,512]{2,1,0:T(8,128)(2,1)}), bf16[128,8,512]{2,1,0:T(8,128)(2,1)S(1)}, u32[]{:S(2)}, u32[]{:S(2)}) async-start(bf16[128,8,512]{2,1,0:T(8,128)(2,1)} %bitcast.121), calls=%async_computation.11 | async-start | bytes 2097152 | tf_op jit(solution)/shard_map/all_to_all | solution.py:610
  343.8 10.2 %collective-permute-start.11 = (f32[4,8,512]{2,1,0:T(8,128)S(1)}, f32[4,8,512]{2,1,0:T(8,128)S(1)}, u32[]{:S(2)}, u32[]{:S(2)}) collective-permute-start(f32[4,8,512]{2,1,0:T(8,128)S(1)} %pad_maximum_fusion.8), channel_id=1, source_target_pairs={{0,32},{8,40},{16,48},{24,56},{32,0},{40,8},{48,16},{56,24},{64,96... | collective-permute-start | bytes 196616 | tf_op jit(solution)/shard_map/ppermute | solution.py:597
  354.0 7.0 %collective-permute-start.12 = (f32[8,8,512]{2,1,0:T(8,128)S(1)}, f32[8,8,512]{2,1,0:T(8,128)S(1)}, u32[]{:S(2)}, u32[]{:S(2)}) collective-permute-start(f32[8,8,512]{2,1,0:T(8,128)S(1)} %pad_maximum_fusion.7), channel_id=1, source_target_pairs={{0,64},{8,72},{16,80},{24,88},{32,96},{40,104},{48,112},{56,120},{... | collective-permute-start | bytes 393224 | tf_op jit(solution)/shard_map/ppermute | solution.py:597
  360.6 5.2 %collective-permute-start.8 = (bf16[8,512]{1,0:T(8,128)(2,1)S(1)}, bf16[8,512]{1,0:T(8,128)(2,1)S(1)}, u32[]{:S(2)}, u32[]{:S(2)}) collective-permute-start(bf16[8,512]{1,0:T(8,128)(2,1)S(1)} %get-tuple-element.114), channel_id=1, source_target_pairs={{0,64},{8,72},{16,80},{24,88},{32,96},{40,104},{48,112},{56,120},{... | collective-permute-start | bytes 24584 | tf_op jit(solution)/shard_map/ppermute | solution.py:589
  366.4 10.1 %all-to-all-start.12 = ((bf16[8,2,8,512]{3,2,1,0:T(8,128)(2,1)}), bf16[8,2,8,512]{3,2,1,0:T(8,128)(2,1)S(1)}, u32[]{:S(2)}, u32[]{:S(2)}) async-start(bf16[8,2,8,512]{3,2,1,0:T(8,128)(2,1)} %broadcast_in_dim.13), calls=%async_computation.12 | async-start | bytes 262144 | tf_op jit(solution)/shard_map/all_to_all | solution.py:579
  (44 other events, 514.7 us)
